TPU v7x, 256 devices: a whole 4x4x8 slice. The times are simulated.
256 devices in a mesh: bead: 32 (over x, z_lo, core), space: 8 (over y, z_hi).
Axes of the slice: x: 4, y: 4, z: 8 (z_hi: 2, z_lo: 4; z = z_hi * 4 + z_lo), core: 2. Of those that a mesh axis runs over, the one named last changes fastest.
Arguments:
- positions: float32 [32, 3, 4096], P('bead', None, 'space'), may hold values from -6 to 6
- momenta: float32 [32, 3, 4096], P('bead', None, 'space'), may hold values from -6 to 6
- species: int32 [4096], P('space'), may hold values from 0 to 1
- neighbours: int32 [8, 4096], P(None, 'space'), may hold values from 0 to 1023
- send_list: int32 [4096], P('space'), may hold values from 0 to 511
- embedding: float32 [2, 128], replicated, may hold values from -4 to 4
- radial_one: float32 [8, 128], replicated, may hold values from -4 to 4
- radial_two: float32 [8, 128], replicated, may hold values from -4 to 4
- mix_one: float32 [128, 384], replicated, may hold values from -0.3125 to 0.3125
- mix_two: float32 [128, 384], replicated, may hold values from -0.3125 to 0.3125
- read_one: float32 [128], replicated, may hold values from -0.5 to 0.5
- read_two: float32 [128], replicated, may hold values from -0.5 to 0.5
Outputs:
- new_positions: float32 [32, 3, 4096], P('bead', None, 'space')
- new_momenta: float32 [32, 3, 4096], P('bead', None, 'space')
Inputs may be any that keep to these rules, and one draw needn't show every extreme that they name: `neighbours`: positions in the extended set of the atom's own domain: below 256 the ghosts from the lower domain, then the 512 own atoms, then the ghosts from the upper domain. `send_list`: entries d * 512 to d * 512 + 255 are sent to domain d - 1, the next 256 to domain d + 1.
All inputs are finite; a program needn't handle non-finite values.
Results may differ from a plain program's by a relative error of at most 0.0003.
Values sent between devices are 32-bit elements; how exact they have to be, the bound alone decides.
A program may use at most 128 MiB of HBM per device.

v0:
```python
import math

import jax
import jax.numpy as jnp
from jax import lax
from jax.sharding import PartitionSpec as P

EXACT = lax.Precision.HIGHEST
STEP = 2.0
HALF_STEP = 1.0
HEAVY = 16.0
SQRT3 = math.sqrt(3.0)
SQRT5 = math.sqrt(5.0)
SQRT15 = math.sqrt(15.0)


def padded(cells, sides, width):
    for axis, dim in sides:
        count = lax.axis_size(axis)
        head = lax.slice_in_dim(cells, 0, width, axis=dim)
        tail = lax.slice_in_dim(cells, cells.shape[dim] - width, cells.shape[dim], axis=dim)
        cells = jnp.concatenate(
            [
                lax.ppermute(tail, axis, [(i, (i + 1) % count) for i in range(count)]),
                cells,
                lax.ppermute(head, axis, [((i + 1) % count, i) for i in range(count)]),
            ],
            axis=dim,
        )
    return cells


def sent_to_all(value, axis):
    copies = jnp.broadcast_to(value, (lax.axis_size(axis), *value.shape))
    return lax.all_to_all(copies, axis, split_axis=0, concat_axis=0, tiled=True)


def joined_along(pieces, dim):
    pieces = jnp.moveaxis(pieces, 0, dim)
    lengths = pieces.shape
    return pieces.reshape(*lengths[:dim], lengths[dim] * lengths[dim + 1], *lengths[dim + 2 :])


def collect(value, axis, dim):
    pieces = sent_to_all(value, axis)
    return joined_along(pieces, dim)


def in_one_piece(arrays, axis, dim, along):
    ends, at = ([], 0)
    for a in arrays[:-1]:
        at += a.shape[along]
        ends.append(at)
    both = jnp.concatenate(arrays, axis=along)
    return tuple(jnp.split(collect(both, axis, dim), ends, axis=along))


def harmonics(unit):
    ux, uy, uz = (unit[0], unit[1], unit[2])
    return jnp.stack(
        [
            jnp.ones_like(ux),
            SQRT3 * ux,
            SQRT3 * uy,
            SQRT3 * uz,
            SQRT15 * ux * uy,
            SQRT15 * uy * uz,
            0.5 * SQRT5 * (2.0 * uz * uz - ux * ux - uy * uy),
            SQRT15 * ux * uz,
            0.5 * SQRT15 * (ux * ux - uy * uy),
        ]
    )


def interaction(ext_coords, centre, slots, ext_feat, radial, mixing):
    neigh_count = slots.shape[0]
    atom_count = slots.shape[1]
    flat_slots = slots.reshape(-1)
    relative = (
        jnp.take(ext_coords, flat_slots, axis=1).reshape(3, neigh_count, atom_count)
        - centre[:, None, :]
    )
    soft_dist = jnp.sqrt(jnp.sum(relative * relative, axis=0) + 1.0)
    sphere = harmonics(relative / soft_dist)
    centres = 1.0 + jnp.arange(radial.shape[0]).astype(jnp.float32)
    basis = jnp.exp(-0.5 * (soft_dist[None] - centres[:, None, None]) ** 2)
    edge_weight = jnp.einsum("nc,nka->cka", radial, basis, precision=EXACT)
    carried = edge_weight * jnp.take(ext_feat, flat_slots, axis=1).reshape(
        -1, neigh_count, atom_count
    )
    moments = jnp.einsum("lka,cka->lca", sphere, carried, precision=EXACT) / neigh_count
    squares = moments * moments
    invariants = jnp.concatenate(
        [squares[0], jnp.sum(squares[1:4], axis=0), jnp.sum(squares[4:9], axis=0)], axis=0
    )
    return jnp.dot(mixing, invariants, precision=EXACT)


def embed(embedding, flags):
    return embedding[0][:, None] + flags[None, :] * (embedding[1] - embedding[0])[:, None]


def normal_modes(bead_total):
    bead_idx = jnp.arange(bead_total).astype(jnp.float32)[:, None]
    mode_idx = jnp.arange(bead_total).astype(jnp.float32)[None, :]
    phase = 2.0 * jnp.pi * bead_idx * mode_idx / bead_total
    half_total = bead_total // 2
    table = jnp.where(
        mode_idx < half_total,
        math.sqrt(2.0 / bead_total) * jnp.cos(phase),
        math.sqrt(2.0 / bead_total) * jnp.sin(phase),
    )
    table = jnp.where(
        mode_idx == half_total, jnp.cos(jnp.pi * bead_idx) / math.sqrt(bead_total), table
    )
    table = jnp.where(mode_idx == 0, 1.0 / math.sqrt(bead_total), table)
    return table


def mode_factors(bead_total):
    mode_idx = jnp.arange(bead_total).astype(jnp.float32)
    angles = float(bead_total) * jnp.sin(jnp.pi * mode_idx / bead_total)
    safe_angles = jnp.where(mode_idx == 0, 1.0, angles)
    cosine = jnp.cos(angles)
    reach = jnp.where(mode_idx == 0, STEP, STEP * jnp.sin(angles) / safe_angles)
    stiff = angles * jnp.sin(angles) / STEP
    return (cosine, reach, stiff)


def shards(
    positions,
    momenta,
    species,
    neighbours,
    send_list,
    embedding,
    radial_one,
    radial_two,
    mix_one,
    mix_two,
    read_one,
    read_two,
):
    atoms_here = neighbours.shape[1]
    ghost_rows = atoms_here // 2
    flags = species.astype(jnp.float32)
    masses = HEAVY - (HEAVY - 1.0) * flags
    own_coords = positions[0]
    own_block = jnp.concatenate([own_coords, flags[None, :]], axis=0)
    outgoing = jnp.take(own_block, send_list, axis=1)
    arrived = padded(outgoing, (("space", 1),), ghost_rows)
    extended = jnp.concatenate(
        [arrived[:, :ghost_rows], own_block, arrived[:, -ghost_rows:]], axis=1
    )
    ext_coords = extended[:3]
    base_ext = embed(embedding, extended[3])
    base_own = base_ext[:, ghost_rows : ghost_rows + atoms_here]

    def first_layer(coords_ext):
        centre = coords_ext[:, ghost_rows : ghost_rows + atoms_here]
        return base_own + jax.nn.silu(
            interaction(coords_ext, centre, neighbours, base_ext, radial_one, mix_one)
        )

    hidden_own, first_back = jax.vjp(first_layer, ext_coords)
    feat_out = jnp.take(hidden_own, send_list, axis=1)
    feat_in = padded(feat_out, (("space", 1),), ghost_rows)
    hidden_ext = jnp.concatenate(
        [feat_in[:, :ghost_rows], hidden_own, feat_in[:, -ghost_rows:]], axis=1
    )

    def second_layer(coords_ext, feat_ext):
        centre = coords_ext[:, ghost_rows : ghost_rows + atoms_here]
        top = interaction(coords_ext, centre, neighbours, feat_ext, radial_two, mix_two)
        own_feat = feat_ext[:, ghost_rows : ghost_rows + atoms_here]
        return jnp.sum(jnp.dot(read_two, jax.nn.silu(top), precision=EXACT)) + jnp.sum(
            jnp.dot(read_one, own_feat, precision=EXACT)
        )

    energy_here, second_back = jax.vjp(second_layer, ext_coords, hidden_ext)
    coord_grad_two, feat_grad = second_back(jnp.ones((), jnp.float32))
    feat_ghost = jnp.concatenate(
        [feat_grad[:, :ghost_rows], feat_grad[:, ghost_rows + atoms_here :]], axis=1
    )
    feat_back = padded(feat_ghost, (("space", 1),), ghost_rows)
    feat_recv = jnp.concatenate([feat_back[:, :ghost_rows], feat_back[:, -ghost_rows:]], axis=1)
    hidden_grad = feat_grad[:, ghost_rows : ghost_rows + atoms_here] + jnp.zeros_like(
        hidden_own
    ).at[:, send_list].add(feat_recv)
    (coord_grad_one,) = first_back(hidden_grad)
    coord_grad = coord_grad_one + coord_grad_two
    coord_ghost = jnp.concatenate(
        [coord_grad[:, :ghost_rows], coord_grad[:, ghost_rows + atoms_here :]], axis=1
    )
    coord_back = padded(coord_ghost, (("space", 1),), ghost_rows)
    coord_recv = jnp.concatenate([coord_back[:, :ghost_rows], coord_back[:, -ghost_rows:]], axis=1)
    own_grad = coord_grad[:, ghost_rows : ghost_rows + atoms_here] + jnp.zeros_like(own_coords).at[
        :, send_list
    ].add(coord_recv)
    kicked = momenta[0] - HALF_STEP * own_grad
    bead_total = lax.axis_size("bead")
    my_bead = lax.axis_index("bead")
    modes_mat = normal_modes(bead_total)
    cosine, reach, stiff = mode_factors(bead_total)
    tables = jnp.stack(
        [
            jnp.einsum("jk,k,bk->jb", modes_mat, cosine, modes_mat, precision=EXACT),
            jnp.einsum("jk,k,bk->jb", modes_mat, reach, modes_mat, precision=EXACT),
            jnp.einsum("jk,k,bk->jb", modes_mat, stiff, modes_mat, precision=EXACT),
        ]
    )
    my_row = lax.dynamic_index_in_dim(tables, my_bead, axis=1, keepdims=False)
    coord_piece, moment_piece = in_one_piece((positions, kicked[None]), "bead", 0, 1)
    rotate_q = jnp.einsum("b,bca->ca", my_row[0], coord_piece, precision=EXACT)
    rotate_p = jnp.einsum("b,bca->ca", my_row[0], moment_piece, precision=EXACT)
    drift = jnp.einsum("b,bca->ca", my_row[1], moment_piece, precision=EXACT)
    spring = jnp.einsum("b,bca->ca", my_row[2], coord_piece, precision=EXACT)
    new_coords = rotate_q + drift / masses[None, :]
    new_moms = rotate_p - masses[None, :] * spring
    return (new_coords[None], new_moms[None])


def solution(mesh):
    placed = (
        P("bead", None, "space"),
        P("bead", None, "space"),
        P("space"),
        P(None, "space"),
        P("space"),
        P(),
        P(),
        P(),
        P(),
        P(),
        P(),
        P(),
    )
    return jax.shard_map(
        shards,
        mesh=mesh,
        in_specs=placed,
        out_specs=(P("bead", None, "space"), P("bead", None, "space")),
        check_vma=False,
    )
```

profile of v0, /device:TPU:1, one launch (start us, length us, event | category | flops | bytes accessed | tf_op | source)
XLA Modules:
  0.0 329.1 jit_solution(6246126397894422187)
XLA Ops:
  3.6 1.0 gather_fusion
  4.8 10.3 %collective-permute-start.1 = (f32[4,256]{0,1:T(8,128)S(1)}, f32[4,256]{0,1:T(8,128)S(1)}, u32[]{:S(2)}, u32[]{:S(2)}) collective-permute-start(f32[4,256]{0,1:T(8,128)S(1)} %get-tuple-element.27), channel_id=1, source_target_pairs={{1,0},{2,1},{3,2},{4,3},{5,4},{6,5},{7,6},{0,7},{9,8},{10,9},{11,1... | collective-permute-start | bytes 12296 | tf_op jit(solution)/shard_map/ppermute | solution.py:26
  15.7 1.3 bitcast_subtract_fusion.3
  17.0 1.2 slice_bitcast_fusion.5
  20.6 0.7 compare_and_fusion.1
  22.0 0.7 copy.299
  25.4 3.9 %collective-permute-done = f32[4,256]{0,1:T(8,128)S(1)} collective-permute-done((f32[4,256]{0,1:T(8,128)S(1)}, f32[4,256]{0,1:T(8,128)S(1)}, u32[]{:S(2)}, u32[]{:S(2)}) %collective-permute-start) | collective-permute-done | bytes 4128 | tf_op jit(solution)/shard_map/ppermute | solution.py:24
  29.6 12.7 %gather_fusion.4 = f32[4096,3]{1,0:T(8,128)S(1)} fusion(f32[3,1024]{0,1:T(8,128)S(1)} %copy.257, s32[4096]{0:T(1024)} %get-tuple-element.39), kind=kCustom, calls=%fused_computation.clone | custom fusion | bytes 114688 | tf_op jit(solution)/shard_map/jvp(jit(_take))/gather | solution.py:80
  43.0 0.8 fusion.89
  44.5 0.8 copy.260
  45.6 14.2 %gather_fusion.1 = f32[4096,128]{1,0:T(8,128)} fusion(f32[128,1024]{0,1:T(8,128)S(1)} %multiply_add_fusion, s32[4096]{0:T(1024)S(1)} %get-tuple-element.48), kind=kCustom, calls=%fused_computation.2 | custom fusion | bytes 4210688 | tf_op jit(solution)/shard_map/jvp(jit(_take))/gather | solution.py:88
  59.8 6.0 %bitcast_multiply_fusion.8 = f32[128,8,512]{0,2,1:T(8,128)S(1)} fusion(f32[128,8,512]{0,2,1:T(8,128)} %bitcast.248, pred[8,512]{1,0:T(8,128)(4,1)S(1)} %compare_and_fusion.1, f32[8]{0:T(128)S(1)} %copy-done.30, f32[8,512]{1,0:T(8,128)S(1)} %sqrt.17, f32[8,128]{1,0:T(8,128)S(1)} %copy-done.29), kind=kOutput, calls=%fused_computation.32 | convolution fusion | flops 51478528 | bytes 4218912 | tf_op jit(solution)/shard_map/jvp(nc,nka->cka)/dot_general | solution.py:87
  65.8 1.3 copy-done.6
  67.1 7.4 %fusion.18 = f32[512,128,9]{1,2,0:T(8,128)S(1)} fusion(f32[9,8,512]{0,1,2:T(8,128)S(1)} %copy.260, f32[128,8,512]{0,2,1:T(8,128)S(1)} %bitcast_multiply_fusion.8), kind=kOutput, calls=%fused_computation.39 | convolution fusion | flops 56623104 | bytes 4603904 | tf_op jit(solution)/shard_map/jvp(lka,cka->lca)/dot_general | solution.py:91
  74.8 1.7 copy-done.1
  76.4 1.4 slice_reduce_fusion.1
  77.9 1.4 slice_reduce_fusion.3
  79.3 0.8 slice.138
  80.1 1.3 div.143
  81.5 2.7 slice_add_fusion
  84.2 2.0 gather_fusion.2
  86.3 3.7 %collective-permute-start.3 = (f32[128,256]{0,1:T(8,128)S(1)}, f32[128,256]{0,1:T(8,128)S(1)}, u32[]{:S(2)}, u32[]{:S(2)}) collective-permute-start(f32[128,256]{0,1:T(8,128)S(1)} %get-tuple-element.25), channel_id=1, source_target_pairs={{1,0},{2,1},{3,2},{4,3},{5,4},{6,5},{7,6},{0,7},{9,8},{10,9},{11,1... | collective-permute-start | bytes 393224 | tf_op jit(solution)/shard_map/ppermute | solution.py:26
  90.0 1.9 collective-permute-start.2
  92.5 1.7 collective-permute-done.3
  94.2 7.8 %collective-permute-done.2 = f32[128,256]{0,1:T(8,128)S(1)} collective-permute-done((f32[128,256]{0,1:T(8,128)S(1)}, f32[128,256]{0,1:T(8,128)S(1)}, u32[]{:S(2)}, u32[]{:S(2)}) %collective-permute-start.2) | collective-permute-done | bytes 131104 | tf_op jit(solution)/shard_map/ppermute | solution.py:24
  102.1 1.0 pad_maximum_fusion
  103.1 14.2 %gather_fusion.3 = f32[4096,128]{1,0:T(8,128)} fusion(f32[128,1024]{0,1:T(8,128)S(1)} %pad_maximum_fusion, s32[4096]{0:T(1024)S(1)} %get-tuple-element.48), kind=kCustom, calls=%fused_computation.4 | custom fusion | bytes 4210688 | tf_op jit(solution)/shard_map/jvp(jit(_take))/gather | solution.py:88
  117.3 5.5 %bitcast_multiply_fusion.7 = (f32[128,8,512]{0,2,1:T(8,128)S(1)}, f32[8,512,128]{2,1,0:T(8,128)S(1)}) fusion(pred[8,512]{1,0:T(8,128)(4,1)S(1)} %compare_and_fusion.1, f32[4096,128]{1,0:T(8,128)} %gather_fusion.3, f32[8,128]{1,0:T(8,128)S(1)} %copy-done.28, f32[8]{0:T(128)S(1)} %copy-done.30, f32[8,512]{1,0:T(8,128)S(1)} %sqrt.17), kind=kOutput, calls=%fused_computation.31 | convolution fusion | flops 51478528 | bytes 6316064 | tf_op jit(solution)/shard_map/jvp(nc,nka->cka)/dot_general | solution.py:87
  122.8 1.3 copy-done.8
  124.1 7.6 %fusion.15 = f32[512,128,9]{1,2,0:T(8,128)S(1)} fusion(f32[9,8,512]{0,1,2:T(8,128)S(1)} %copy.260, f32[128,8,512]{0,2,1:T(8,128)S(1)} %get-tuple-element.46), kind=kOutput, calls=%fused_computation.36 | convolution fusion | flops 56623104 | bytes 4603904 | tf_op jit(solution)/shard_map/jvp(lka,cka->lca)/dot_general | solution.py:91
  132.8 0.7 slice_reduce_fusion.2
  133.6 0.8 fusion.45
  134.5 0.8 convolution_bitcast_fusion.1
  135.8 6.7 %fusion.6 = f32[512,128,8]{1,2,0:T(8,128)S(1)} fusion(f32[9,8,512]{0,1,2:T(8,128)S(1)} %copy.260, f32[1,128,512]{1,0,2:T(1,128)S(1)} %bitcast.256, f32[3,128,512]{1,0,2:T(4,128)S(1)} %broadcast_in_dim.216, f32[5,128,512]{1,0,2:T(8,128)S(1)} %broadcast_in_dim.215, f32[512,128,9]{1,2,0:T(8,128)S(1)} %fusion.15), kind=kOutput, calls=%fused_computation.16 | convolution fusion | flops 60162048 | bytes 6963200 | tf_op jit(solution)/shard_map/transpose(jvp(lka,cka->lca))/dot_general | solution.py:91
  142.5 2.0 bitcast_multiply_fusion.5
  144.4 23.3 %scatter_fusion = f32[128,1024]{0,1:T(8,128)S(1)} fusion(f32[128,1024]{0,1:T(8,128)S(1)} %pad.45, s32[4096]{0:T(1024)S(1)} %bitcast.282, f32[4096,128]{1,0:T(8,128)} %bitcast.251), kind=kCustom, calls=%fused_computation.5 | custom fusion | flops 524288 | bytes 6307840 | tf_op jit(solution)/shard_map/transpose(jvp(jit(_take)))/scatter-add | solution.py:88
  167.7 0.7 fusion.189
  168.5 13.6 %fusion.4 = f32[512,9,8]{1,2,0:T(8,128)} fusion(f32[128,8,512]{0,2,1:T(8,128)} %copy-done.8, f32[1,128,512]{1,0,2:T(1,128)S(1)} %bitcast.257, f32[3,128,512]{1,0,2:T(4,128)} %copy-done.13, f32[5,128,512]{1,0,2:T(8,128)} %copy-done.9, f32[512,128,9]{1,2,0:T(8,128)} %copy-done.3), kind=kOutput, calls=%fused_computation.14 | convolution fusion | flops 60162048 | bytes 6963200 | tf_op jit(solution)/shard_map/transpose(jvp(lka,cka->lca))/dot_general | solution.py:91
  182.1 3.5 %fusion.34 = f32[8,512]{1,0:T(8,128)} fusion(f32[512,128,8]{1,2,0:T(8,128)S(1)} %copy-done.5, f32[128,8,512]{0,2,1:T(8,128)S(1)} %bitcast.250, pred[8,512]{1,0:T(8,128)(4,1)S(1)} %compare_and_fusion.1, f32[8]{0:T(128)S(1)} %copy-done.30, f32[8,512]{1,0:T(8,128)S(1)} %sqrt.17, f32[8,128]{1,0:T(8,128)S(1)} %copy-done.28), kind=kOutput, calls=%fused_computation.54 | convolution fusion | flops 51638272 | bytes 4235296 | tf_op jit(solution)/shard_map/transpose(jvp(nc,nka->cka))/dot_general | solution.py:87
  185.6 1.1 collective-permute-start.5
  186.7 4.3 %collective-permute-start.4 = (f32[128,256]{0,1:T(8,128)}, f32[128,256]{0,1:T(8,128)S(1)}, u32[]{:S(2)}, u32[]{:S(2)}) collective-permute-start(f32[128,256]{0,1:T(8,128)} %get-tuple-element.22), channel_id=1, source_target_pairs={{0,1},{1,2},{2,3},{3,4},{4,5},{5,6},{6,7},{7,0},{8,9},{9,10},{10,1... | collective-permute-start | bytes 393224 | tf_op jit(solution)/shard_map/ppermute | solution.py:24
  191.0 2.2 copy.275
  193.6 6.3 %collective-permute-done.4 = f32[128,256]{0,1:T(8,128)S(1)} collective-permute-done((f32[128,256]{0,1:T(8,128)}, f32[128,256]{0,1:T(8,128)S(1)}, u32[]{:S(2)}, u32[]{:S(2)}) %collective-permute-start.4) | collective-permute-done | bytes 131104 | tf_op jit(solution)/shard_map/ppermute | solution.py:24
  199.9 3.6 %scatter_custom_fusion.1 = f32[128,512]{0,1:T(8,128)S(1)} fusion(f32[128,512]{0,1:T(8,128)S(1)} %slice.146, s32[512]{0:T(512)S(1)} %compare_select_fusion.3, f32[128,256]{0,1:T(8,128)S(1)} %collective-permute-done.5, f32[]{:T(128)} %constant.178, f32[128,256]{0,1:T(8,128)S(1)} %collective-permute-done.4), kind=kCustom, calls=%fused_computation.87 | custom fusion | flops 131072 | bytes 524292 | tf_op jit(solution)/shard_map/scatter-add | solution.py:189
  203.6 0.8 convolution_bitcast_fusion
  204.8 0.9 copy-done.14
  205.7 1.3 copy-done.10
  207.1 0.8 copy-done.2
  207.9 9.9 %fusion.2 = f32[512,9,8]{1,2,0:T(8,128)} fusion(f32[128,8,512]{0,2,1:T(8,128)S(1)} %copy-done.7, f32[1,128,512]{1,0,2:T(1,128)S(1)} %bitcast.258, f32[3,128,512]{1,0,2:T(4,128)S(1)} %broadcast_in_dim.219, f32[5,128,512]{1,0,2:T(8,128)S(1)} %broadcast_in_dim.218, f32[512,128,9]{1,2,0:T(8,128)S(1)} %copy-done.2), kind=kOutput, calls=%fused_computation.12 | convolution fusion | flops 60162048 | bytes 6963200 | tf_op jit(solution)/shard_map/transpose(jvp(lka,cka->lca))/dot_general | solution.py:91
  217.7 2.3 copy.266
  220.1 8.6 %fusion = f32[512,128,8]{1,2,0:T(8,128)S(1)} fusion(f32[9,8,512]{0,1,2:T(8,128)S(1)} %copy.260, f32[1,128,512]{1,0,2:T(1,128)S(1)} %bitcast.259, f32[3,128,512]{1,0,2:T(4,128)} %copy-done.14, f32[5,128,512]{1,0,2:T(8,128)} %copy-done.10, f32[512,128,9]{1,2,0:T(8,128)} %copy-done.1), kind=kOutput, calls=%fused_computation.10 | convolution fusion | flops 60162048 | bytes 6963200 | tf_op jit(solution)/shard_map/transpose(jvp(lka,cka->lca))/dot_general | solution.py:91
  228.7 2.9 fusion.35
  231.7 0.8 fusion.184
  233.7 2.0 copy.280
  235.7 22.6 %scatter_fusion.1 = f32[3,1024]{0,1:T(8,128)S(1)} fusion(f32[3,1024]{0,1:T(8,128)S(1)} %pad.55, s32[4096]{0:T(1024)S(1)} %get-tuple-element.38, f32[4096,3]{1,0:T(8,128)S(1)} %copy.273), kind=kCustom, calls=%fused_computation.7 | custom fusion | flops 12288 | bytes 163840 | tf_op jit(solution)/shard_map/transpose(jvp(jit(_take)))/scatter-add | solution.py:80
  258.2 22.9 %scatter_fusion.2 = f32[3,1024]{0,1:T(8,128)S(1)} fusion(f32[3,1024]{0,1:T(8,128)S(1)} %pad.59, s32[4096]{0:T(1024)S(1)} %get-tuple-element.38, f32[4096,3]{1,0:T(8,128)} %copy.280), kind=kCustom, calls=%fused_computation.8 | custom fusion | flops 12288 | bytes 163840 | tf_op jit(solution)/shard_map/transpose(jvp(jit(_take)))/scatter-add | solution.py:80
  281.3 1.4 collective-permute-start.7
  282.7 4.0 %collective-permute-start.6 = (f32[3,256]{0,1:T(8,128)S(1)}, f32[3,256]{0,1:T(8,128)S(1)}, u32[]{:S(2)}, u32[]{:S(2)}) collective-permute-start(f32[3,256]{0,1:T(8,128)S(1)} %get-tuple-element.20), channel_id=1, source_target_pairs={{0,1},{1,2},{2,3},{3,4},{4,5},{5,6},{6,7},{7,0},{8,9},{9,10},{10,1... | collective-permute-start | bytes 9224 | tf_op jit(solution)/shard_map/ppermute | solution.py:24
  287.0 2.3 collective-permute-done.7
  289.3 10.6 %collective-permute-done.6 = f32[3,256]{0,1:T(8,128)S(1)} collective-permute-done((f32[3,256]{0,1:T(8,128)S(1)}, f32[3,256]{0,1:T(8,128)S(1)}, u32[]{:S(2)}, u32[]{:S(2)}) %collective-permute-start.6) | collective-permute-done | bytes 3104 | tf_op jit(solution)/shard_map/ppermute | solution.py:24
  300.1 3.7 %scatter_fusion.3 = f32[3,512]{0,1:T(8,128)S(1)} fusion(f32[3,512]{0,1:T(8,128)S(1)} %slice.149, s32[512]{0:T(512)S(1)} %compare_select_fusion.3, f32[512,3]{1,0:T(8,128)S(1)} %copy.283), kind=kCustom, calls=%fused_computation.9 | custom fusion | flops 1536 | bytes 20480 | tf_op jit(solution)/shard_map/scatter-add | solution.py:199
  304.0 1.0 broadcast_in_dim.224
  305.0 7.6 %all-to-all-start = ((f32[32,1,6,512]{3,1,2,0:T(1,128)}), f32[32,1,6,512]{3,1,2,0:T(1,128)S(1)}, u32[]{:S(2)}, u32[]{:S(2)}) async-start(f32[32,1,6,512]{3,1,2,0:T(1,128)} %broadcast_in_dim.224), calls=%async_computation | async-start | bytes 786432 | tf_op jit(solution)/shard_map/all_to_all | solution.py:35
  313.8 12.8 %all-to-all-done = f32[32,1,6,512]{3,1,2,0:T(1,128)S(1)} async-done(((f32[32,1,6,512]{3,1,2,0:T(1,128)}), f32[32,1,6,512]{3,1,2,0:T(1,128)S(1)}, u32[]{:S(2)}, u32[]{:S(2)}) %all-to-all-start) | async-done | bytes 393248 | tf_op jit(solution)/shard_map/all_to_all | solution.py:35
  (183 shorter events, 19.9 us)
Async XLA Ops:
  0.6 80.8 %copy-start = (f32[128,384]{1,0:T(8,128)S(1)}, f32[128,384]{1,0:T(8,128)}, u32[]{:S(2)}) copy-start(f32[128,384]{1,0:T(8,128)} %param.22) | copy-start | bytes 589828
  2.1 21.3 %copy-start.33 = (pred[512]{0:T(512)(128)(4,1)}, pred[512]{0:T(512)(128)(4,1)S(1)}, u32[]{:S(2)}) copy-start(pred[512]{0:T(512)(128)(4,1)S(1)} %compare_and_fusion.2) | copy-start | bytes 1540
  3.6 19.8 %copy-start.26 = (s32[1024]{0:T(1024)}, s32[1024]{0:T(1024)S(1)}, u32[]{:S(2)}) copy-start(s32[1024]{0:T(1024)S(1)} %pad_clamp_fusion) | copy-start | bytes 12292
  4.8 20.4 %collective-permute-start.1 = (f32[4,256]{0,1:T(8,128)S(1)}, f32[4,256]{0,1:T(8,128)S(1)}, u32[]{:S(2)}, u32[]{:S(2)}) collective-permute-start(f32[4,256]{0,1:T(8,128)S(1)} %get-tuple-element.27), channel_id=1, source_target_pairs={{1,0},{2,1},{3,2},{4,3},{5,4},{6,5},{7,6},{0,7},{9,8},{10,9},{11,1... | collective-permute-start | bytes 12296 | tf_op jit(solution)/shard_map/ppermute | solution.py:26
  15.1 14.1 %collective-permute-start = (f32[4,256]{0,1:T(8,128)S(1)}, f32[4,256]{0,1:T(8,128)S(1)}, u32[]{:S(2)}, u32[]{:S(2)}) collective-permute-start(f32[4,256]{0,1:T(8,128)S(1)} %get-tuple-element.26), channel_id=1, source_target_pairs={{0,1},{1,2},{2,3},{3,4},{4,5},{5,6},{6,7},{7,0},{8,9},{9,10},{10,1... | collective-permute-start | bytes 12296 | tf_op jit(solution)/shard_map/ppermute | solution.py:24
  42.3 2.1 copy-start.19
  42.3 3.0 copy-start.35
  42.3 3.0 copy-start.36
  45.5 14.2 %copy-start.29 = (f32[8,128]{1,0:T(8,128)S(1)}, f32[8,128]{1,0:T(8,128)}, u32[]{:S(2)}) copy-start(f32[8,128]{1,0:T(8,128)} %param.20) | copy-start | bytes 12292
  45.6 14.2 %copy-start.30 = (f32[8]{0:T(128)S(1)}, f32[8]{0:T(128)}, u32[]{:S(2)}) copy-start(f32[8]{0:T(128)} %convert_add_fusion) | copy-start | bytes 100
  65.8 1.3 copy-start.6
  74.5 1.9 copy-start.1
  77.9 6.3 %copy-start.27 = (s32[1024]{0:T(1024)S(1)}, s32[1024]{0:T(1024)}, u32[]{:S(2)}) copy-start(s32[1024]{0:T(1024)} %copy-done.26) | copy-start | bytes 12292
  81.5 4.7 %copy-start.34 = (pred[512]{0:T(512)(128)(4,1)S(1)}, pred[512]{0:T(512)(128)(4,1)}, u32[]{:S(2)}) copy-start(pred[512]{0:T(512)(128)(4,1)} %copy-done.33) | copy-start | bytes 1540
  86.3 7.9 %collective-permute-start.3 = (f32[128,256]{0,1:T(8,128)S(1)}, f32[128,256]{0,1:T(8,128)S(1)}, u32[]{:S(2)}, u32[]{:S(2)}) collective-permute-start(f32[128,256]{0,1:T(8,128)S(1)} %get-tuple-element.25), channel_id=1, source_target_pairs={{1,0},{2,1},{3,2},{4,3},{5,4},{6,5},{7,6},{0,7},{9,8},{10,9},{11,1... | collective-permute-start | bytes 393224 | tf_op jit(solution)/shard_map/ppermute | solution.py:26
  90.0 12.0 %collective-permute-start.2 = (f32[128,256]{0,1:T(8,128)S(1)}, f32[128,256]{0,1:T(8,128)S(1)}, u32[]{:S(2)}, u32[]{:S(2)}) collective-permute-start(f32[128,256]{0,1:T(8,128)S(1)} %get-tuple-element.24), channel_id=1, source_target_pairs={{0,1},{1,2},{2,3},{3,4},{4,5},{5,6},{6,7},{7,0},{8,9},{9,10},{10,1... | collective-permute-start | bytes 393224 | tf_op jit(solution)/shard_map/ppermute | solution.py:24
  103.0 14.2 %copy-start.28 = (f32[8,128]{1,0:T(8,128)S(1)}, f32[8,128]{1,0:T(8,128)}, u32[]{:S(2)}) copy-start(f32[8,128]{1,0:T(8,128)} %param.21) | copy-start | bytes 12292
  122.8 1.3 copy-start.8
  131.7 4.0 %copy-start.3 = (f32[512,128,9]{1,2,0:T(8,128)}, f32[512,128,9]{1,2,0:T(8,128)S(1)}, u32[]{:S(2)}) copy-start(f32[512,128,9]{1,2,0:T(8,128)S(1)} %fusion.15) | copy-start | bytes 7077892
  132.0 1.6 copy-start.18
  132.7 1.7 copy-start.37
  135.6 6.8 %copy-start.13 = (f32[3,128,512]{1,0,2:T(4,128)}, f32[3,128,512]{1,0,2:T(4,128)S(1)}, u32[]{:S(2)}) copy-start(f32[3,128,512]{1,0,2:T(4,128)S(1)} %broadcast_in_dim.216) | copy-start | bytes 2359300
  135.8 6.7 %copy-start.9 = (f32[5,128,512]{1,0,2:T(8,128)}, f32[5,128,512]{1,0,2:T(8,128)S(1)}, u32[]{:S(2)}) copy-start(f32[5,128,512]{1,0,2:T(8,128)S(1)} %broadcast_in_dim.215) | copy-start | bytes 3932164
  142.4 2.0 copy-start.4
  168.5 13.6 %copy-start.5 = (f32[512,128,8]{1,2,0:T(8,128)S(1)}, f32[512,128,8]{1,2,0:T(8,128)}, u32[]{:S(2)}) copy-start(f32[512,128,8]{1,2,0:T(8,128)} %copy-done.4) | copy-start | bytes 6291460
  168.5 13.6 %copy-start.12 = (f32[4096,128]{1,0:T(8,128)S(1)}, f32[4096,128]{1,0:T(8,128)}, u32[]{:S(2)}) copy-start(f32[4096,128]{1,0:T(8,128)} %gather_fusion.3) | copy-start | bytes 6291460
  185.6 17.9 %copy-start.17 = (f32[128,512]{0,1:T(8,128)S(1)}, f32[128,512]{0,1:T(8,128)}, u32[]{:S(2)}) copy-start(f32[128,512]{0,1:T(8,128)} %get-tuple-element.45) | copy-start | bytes 786436
  185.6 8.0 %collective-permute-start.5 = (f32[128,256]{0,1:T(8,128)}, f32[128,256]{0,1:T(8,128)S(1)}, u32[]{:S(2)}, u32[]{:S(2)}) collective-permute-start(f32[128,256]{0,1:T(8,128)} %get-tuple-element.23), channel_id=1, source_target_pairs={{1,0},{2,1},{3,2},{4,3},{5,4},{6,5},{7,6},{0,7},{9,8},{10,9},{11,1... | collective-permute-start | bytes 393224 | tf_op jit(solution)/shard_map/ppermute | solution.py:26
  186.7 13.2 %collective-permute-start.4 = (f32[128,256]{0,1:T(8,128)}, f32[128,256]{0,1:T(8,128)S(1)}, u32[]{:S(2)}, u32[]{:S(2)}) collective-permute-start(f32[128,256]{0,1:T(8,128)} %get-tuple-element.22), channel_id=1, source_target_pairs={{0,1},{1,2},{2,3},{3,4},{4,5},{5,6},{6,7},{7,0},{8,9},{9,10},{10,1... | collective-permute-start | bytes 393224 | tf_op jit(solution)/shard_map/ppermute | solution.py:24
  193.2 10.3 %copy-start.15 = (f32[512,9,8]{0,2,1:T(8,128)}, f32[512,9,8]{0,2,1:T(8,128)S(1)}, u32[]{:S(2)}) copy-start(f32[512,9,8]{0,2,1:T(8,128)S(1)} %copy.275) | copy-start | bytes 442372
  193.2 38.3 %copy-start.20 = (f32[1,8,512]{2,1,0:T(8,128)}, f32[1,8,512]{2,1,0:T(8,128)S(1)}, u32[]{:S(2)}) copy-start(f32[1,8,512]{2,1,0:T(8,128)S(1)} %get-tuple-element.30) | copy-start | bytes 49156
  193.2 38.3 %copy-start.21 = (f32[1,8,512]{2,1,0:T(8,128)}, f32[1,8,512]{2,1,0:T(8,128)S(1)}, u32[]{:S(2)}) copy-start(f32[1,8,512]{2,1,0:T(8,128)S(1)} %get-tuple-element.31) | copy-start | bytes 49156
  203.6 3.5 %copy-start.7 = (f32[128,8,512]{0,2,1:T(8,128)S(1)}, f32[128,8,512]{0,2,1:T(8,128)}, u32[]{:S(2)}) copy-start(f32[128,8,512]{0,2,1:T(8,128)} %copy-done.6) | copy-start | bytes 6291460
  204.4 3.5 %copy-start.2 = (f32[512,128,9]{1,2,0:T(8,128)S(1)}, f32[512,128,9]{1,2,0:T(8,128)}, u32[]{:S(2)}) copy-start(f32[512,128,9]{1,2,0:T(8,128)} %copy-done.1) | copy-start | bytes 7077892
  204.7 1.0 copy-start.14
  205.7 1.4 copy-start.10
  217.7 2.3 copy-start.16
  220.1 8.6 %copy-start.11 = (f32[4096,128]{1,0:T(8,128)S(1)}, f32[4096,128]{1,0:T(8,128)}, u32[]{:S(2)}) copy-start(f32[4096,128]{1,0:T(8,128)} %gather_fusion.1) | copy-start | bytes 6291460
  228.6 2.9 copy-start.24
  228.6 3.0 copy-start.22
  228.7 3.0 copy-start.23
  235.7 51.1 %copy-start.32 = (f32[1,3,512]{2,0,1:T(1,128)S(1)}, f32[1,3,512]{2,0,1:T(1,128)}, u32[]{:S(2)}) copy-start(f32[1,3,512]{2,0,1:T(1,128)} %param.15) | copy-start | bytes 18436
  281.1 22.8 %copy-start.25 = (f32[1,3,512]{2,0,1:T(1,128)S(1)}, f32[1,3,512]{2,0,1:T(1,128)}, u32[]{:S(2)}) copy-start(f32[1,3,512]{2,0,1:T(1,128)} %param.14) | copy-start | bytes 18436
  281.2 31.5 %copy-start.38 = (f32[32]{0:T(128)S(1)}, f32[32]{0:T(128)}, u32[]{:S(2)}) copy-start(f32[32]{0:T(128)} %get-tuple-element.50) | copy-start | bytes 388
  281.2 31.5 %copy-start.39 = (f32[32]{0:T(128)S(1)}, f32[32]{0:T(128)}, u32[]{:S(2)}) copy-start(f32[32]{0:T(128)} %get-tuple-element.54) | copy-start | bytes 388
  281.2 31.5 %copy-start.40 = (pred[32]{0:T(512)(128)(4,1)S(1)}, pred[32]{0:T(512)(128)(4,1)}, u32[]{:S(2)}) copy-start(pred[32]{0:T(512)(128)(4,1)} %get-tuple-element.51) | copy-start | bytes 100
  281.2 31.5 %copy-start.41 = (pred[32]{0:T(512)(128)(4,1)S(1)}, pred[32]{0:T(512)(128)(4,1)}, u32[]{:S(2)}) copy-start(pred[32]{0:T(512)(128)(4,1)} %get-tuple-element.52) | copy-start | bytes 100
  281.2 31.5 %copy-start.42 = (f32[32]{0:T(128)S(1)}, f32[32]{0:T(128)}, u32[]{:S(2)}) copy-start(f32[32]{0:T(128)} %get-tuple-element.49) | copy-start | bytes 388
  281.2 31.5 %copy-start.44 = (f32[32]{0:T(128)S(1)}, f32[32]{0:T(128)}, u32[]{:S(2)}) copy-start(f32[32]{0:T(128)} %iota_convert_fusion) | copy-start | bytes 388
  281.3 31.8 %copy-start.43 = (f32[32]{0:T(128)S(1)}, f32[32]{0:T(128)}, u32[]{:S(2)}) copy-start(f32[32]{0:T(128)} %get-tuple-element.53) | copy-start | bytes 388
  281.3 7.9 %collective-permute-start.7 = (f32[3,256]{0,1:T(8,128)S(1)}, f32[3,256]{0,1:T(8,128)S(1)}, u32[]{:S(2)}, u32[]{:S(2)}) collective-permute-start(f32[3,256]{0,1:T(8,128)S(1)} %get-tuple-element.21), channel_id=1, source_target_pairs={{1,0},{2,1},{3,2},{4,3},{5,4},{6,5},{7,6},{0,7},{9,8},{10,9},{11,1... | collective-permute-start | bytes 9224 | tf_op jit(solution)/shard_map/ppermute | solution.py:26
  282.7 17.2 %collective-permute-start.6 = (f32[3,256]{0,1:T(8,128)S(1)}, f32[3,256]{0,1:T(8,128)S(1)}, u32[]{:S(2)}, u32[]{:S(2)}) collective-permute-start(f32[3,256]{0,1:T(8,128)S(1)} %get-tuple-element.20), channel_id=1, source_target_pairs={{0,1},{1,2},{2,3},{3,4},{4,5},{5,6},{6,7},{7,0},{8,9},{9,10},{10,1... | collective-permute-start | bytes 9224 | tf_op jit(solution)/shard_map/ppermute | solution.py:24
  286.9 26.9 %copy-start.31 = (s32[512]{0:T(512)S(1)}, s32[512]{0:T(512)}, u32[]{:S(2)}) copy-start(s32[512]{0:T(512)} %param.16) | copy-start | bytes 6148
  305.0 21.7 %all-to-all-start = ((f32[32,1,6,512]{3,1,2,0:T(1,128)}), f32[32,1,6,512]{3,1,2,0:T(1,128)S(1)}, u32[]{:S(2)}, u32[]{:S(2)}) async-start(f32[32,1,6,512]{3,1,2,0:T(1,128)} %broadcast_in_dim.224), calls=%async_computation | async-start | bytes 786432 | tf_op jit(solution)/shard_map/all_to_all | solution.py:35
where the time goes:
time: 335 us; the launch traced here: 329 us
  other arithmetic  95.8 us (29%)
  matrix products  78.6 us (23%)
  local copies, waits for them, and re-layouts  72.6 us (22%)
  waiting for transfers between devices  45.7 us (14%)
  starting transfers between devices  34.3 us (10%)
    dot_general x6, matrix products, interaction(): jnp.einsum('lka,cka->lca', sphere, carried, precision=EXACT) / neigh_count  53.6 us
    scatter-add x2, other arithmetic, interaction(): jnp.take(ext_coords, flat_slots, axis=1).reshape(3, neigh_count, atom_count)  45.4 us
    ppermute x4, waiting for transfers between devices, padded(): lax.ppermute(tail, axis, [(i, (i + 1) % count) for i in range(count)])  28.6 us
    gather x2, local copies, waits for them, and re-layouts, interaction(): jnp.take(ext_feat, flat_slots, axis=1).reshape(-1, neigh_count, atom_count)  28.4 us
    scatter-add x1, other arithmetic, interaction(): jnp.take(ext_feat, flat_slots, axis=1).reshape(-1, neigh_count, atom_count)  23.3 us
    dot_general x4, matrix products, interaction(): edge_weight = jnp.einsum('nc,nka->cka', radial, basis, precision=EXACT)  17.9 us
    ppermute x4, starting transfers between devices, padded(): lax.ppermute(head, axis, [((i + 1) % count, i) for i in range(count)])  16.5 us
    gather x2, local copies, waits for them, and re-layouts, interaction(): jnp.take(ext_coords, flat_slots, axis=1).reshape(3, neigh_count, atom_count)  13.3 us
  transfers between devices with their start and end apart: 9, of which 8 were waited for; matrix products, arithmetic and copies ran while one was open for 4% of the time, Pallas kernels for 0%

commit v1 on v0

v1 whole, which is shorter than its diff:
```python
import math

import numpy as np

import jax
import jax.numpy as jnp
from jax import lax
from jax.experimental import pallas as pl
from jax.experimental.pallas import tpu as pltpu
from jax.sharding import PartitionSpec as P

STEP = 2.0
HEAVY = 16.0
SQRT3 = math.sqrt(3.0)
SQRT5 = math.sqrt(5.0)
SQRT15 = math.sqrt(15.0)
F32 = jnp.float32
BF16 = jnp.bfloat16
I32 = jnp.int32
NT = (((1,), (1,)), ((), ()))
VM = pl.BlockSpec(memory_space=pltpu.VMEM)
SM = pl.BlockSpec(memory_space=pltpu.SMEM)
MESH = pl.DeviceIdType.MESH


def dot(a, b):
    return jnp.dot(a, b, preferred_element_type=F32)


def dot_nt(a, b):
    return lax.dot_general(a, b, NT, preferred_element_type=F32)


def split(x):
    hi = x.astype(BF16)
    return hi, (x - hi.astype(F32)).astype(BF16)


def halves(x):
    n = x.shape[0] // 2
    return x[:n] + x[n:]


def lane_take(tiles, idx):
    low = idx & 127
    high = idx >> 7
    out = jnp.take_along_axis(tiles[0], low, axis=1)
    for t in range(1, len(tiles)):
        out = jnp.where(high == t, jnp.take_along_axis(tiles[t], low, axis=1), out)
    return out


def spread(row, count=8):
    return jnp.broadcast_to(row, (count, row.shape[1]))


def tiles_of(ref, first):
    return [ref[first : first + 8, t * 128 : (t + 1) * 128] for t in range(4)]


def compute_kernel(
    own, low1, up1, low2, up2, emb, r1, r2, mix1, mix2, rd1, rd2,
    to_low, to_up, to_low2, to_up2, kept,
    nb_s, geo, yy, bb, hot, m1, hs, ds1, gg, ww, m2, dg, dw, part, two, dh, dr, fl,
):
    def send_of(ref):
        return ref[4:5, :].astype(I32)

    sends = [send_of(r) for r in (own, low1, up1, low2, up2)]

    def slots(ref, send, half, first=0):
        tiles = tiles_of(ref, first)
        out = []
        for t in range(2):
            at = half * 256 + t * 128
            out.append(lane_take(tiles, spread(send[:, at : at + 128])))
        return out

    own_t = tiles_of(own, 0)
    ext_own = slots(low1, sends[1], 1) + own_t + slots(up1, sends[2], 0)
    ext_low = slots(low2, sends[3], 1) + tiles_of(low1, 0) + slots(own, sends[0], 0)
    ext_up = slots(own, sends[0], 1) + tiles_of(up1, 0) + slots(up2, sends[4], 0)
    nb_t = slots(low1, sends[1], 1, 8) + tiles_of(own, 8) + slots(up1, sends[2], 0, 8)
    nb_t = [x.astype(I32) for x in nb_t]

    for e in range(8):
        cols = slice(e * 128, (e + 1) * 128)
        ext = ext_low if e < 2 else (ext_own if e < 6 else ext_up)
        idx = nb_t[e]
        nb_s[:, cols] = idx
        fl[:, cols] = spread(ext_own[e][3:4])
        got = [lane_take([spread(x[c : c + 1]) for x in ext], idx) for c in range(4)]
        rx, ry, rz = [got[c] - spread(ext_own[e][c : c + 1]) for c in range(3)]
        s = jnp.sqrt(rx * rx + ry * ry + rz * rz + 1.0)
        inv = 1.0 / s
        ux, uy, uz = rx * inv, ry * inv, rz * inv
        for c, v in enumerate((ux, uy, uz, s, inv, got[3])):
            geo[c, :, cols] = v
        ys = (
            SQRT3 * ux, SQRT3 * uy, SQRT3 * uz,
            SQRT15 * ux * uy, SQRT15 * uy * uz,
            0.5 * SQRT5 * (2.0 * uz * uz - ux * ux - uy * uy),
            SQRT15 * ux * uz, 0.5 * SQRT15 * (ux * ux - uy * uy),
        )
        for l in range(8):
            yy[l, :, cols] = ys[l]
        for n in range(8):
            bb[n, :, cols] = jnp.exp(-0.5 * (s - (1.0 + n)) ** 2)

    @pl.loop(0, 8)
    def _(rc):
        at = pl.multiple_of(rc * 128, 128)
        ids = lax.broadcasted_iota(I32, (128, 512), 0) + at
        for k in range(8):
            row = jnp.broadcast_to(nb_s[k : k + 1, 256:768], (128, 512))
            hot[pl.ds(at, 128), k * 512 : (k + 1) * 512] = jnp.where(ids == row, 1.0, 0.0).astype(BF16)

    w_rows = []
    for f in range(2):
        for n in range(8):
            w_rows.append(spread(r1[n : n + 1, :] * emb[f : f + 1, :] * 0.125))
    wt = jnp.concatenate(w_rows, axis=0)
    wth, wtl = split(wt)
    wh, wl = split(jnp.transpose(wt))
    zero = jnp.zeros((128, 128), BF16)
    wf = jnp.concatenate([jnp.concatenate([wh, wh], 1), jnp.concatenate([wl, zero], 1)], 0)
    wtf = jnp.concatenate([jnp.concatenate([wth, wth], 1), jnp.concatenate([wtl, zero], 1)], 0)
    r2s = r2[...] * 0.125
    rows = jnp.concatenate([emb[...], rd1[...], rd2[...], jnp.zeros((4, 128), F32), r2s], 0)
    colmat = jnp.transpose(jnp.concatenate([rows, jnp.zeros((112, 128), F32)], 0))
    e0, e1 = colmat[:, 0:1], colmat[:, 1:2]
    c_rd1, c_rd2 = colmat[:, 2:3], colmat[:, 3:4]
    m1h, m1l = split(mix1[...])
    m1s = jnp.concatenate([m1h, m1l], 0)
    m1t = jnp.transpose(mix1[...])
    m1th, m1tl = split(m1t)
    m1ts = jnp.concatenate([m1th, m1tl], 0)
    m2h, m2l = split(mix2[...])
    m2s = jnp.concatenate([m2h, m2l], 0)
    m2th, m2tl = split(jnp.transpose(mix2[...]))
    m2ts = jnp.concatenate([m2th, m2tl], 0)

    def mixed(ws, wh_, x):
        hi, lo = split(x)
        return halves(dot(ws, hi)) + dot(wh_, lo)

    @pl.loop(0, 4)
    def _(ch):
        sl = pl.ds(pl.multiple_of(ch * 256, 256), 256)
        f = geo[5, :, sl]
        bs = []
        for n in range(8):
            bs.append(bb[n, :, sl] * (1.0 - f))
        for n in range(8):
            bs.append(bb[n, :, sl] * f)
        q = [None, None, None]
        for l in range(9):
            z = jnp.concatenate(bs if l == 0 else [yy[l - 1, :, sl] * b for b in bs], 0)
            m = halves(dot(wf, jnp.concatenate(split(z), 0)))
            m1[l, :, sl] = m
            g = 0 if l == 0 else (1 if l < 4 else 2)
            q[g] = m * m if q[g] is None else q[g] + m * m
        v = mixed(m1s, m1h, jnp.concatenate(q, 0))
        sg = 1.0 / (1.0 + jnp.exp(-v))
        fc = fl[0:1, sl]
        h = e0 + fc * (e1 - e0) + v * sg
        ds1[:, sl] = sg * (1.0 + v * (1.0 - sg))
        hs[:, sl] = jnp.concatenate(split(h), 0)

    own_lanes = slice(256, 768)
    iota8 = lax.broadcasted_iota(I32, (8, 512), 0).astype(F32)
    r2th, r2tl = split(colmat[:, 8:16])
    r2lhs = jnp.concatenate([r2th.astype(F32), r2th.astype(F32), r2tl.astype(F32)], 1).astype(BF16)

    def basis(k):
        off = spread(geo[3, k : k + 1, own_lanes]) - 1.0 - iota8
        return off, jnp.exp(-0.5 * off * off)

    for k in range(8):
        gg[k] = halves(dot(hs[...], hot[:, k * 512 : (k + 1) * 512]))
        _, bk = basis(k)
        bh, bl = split(bk)
        rhs = jnp.concatenate([bh.astype(F32), bl.astype(F32), bh.astype(F32)], 0).astype(BF16)
        ww[k] = dot(r2lhs, rhs)

    def y_row(l, k, it):
        at = pl.multiple_of(256 + it * 128, 128)
        return yy[l - 1, k : k + 1, pl.ds(at, 128)]

    @pl.loop(0, 16)
    def _(step):
        it = step // 4
        rows_ = pl.ds(pl.multiple_of((step % 4) * 32, 32), 32)
        lanes = pl.ds(pl.multiple_of(it * 128, 128), 128)
        car = [gg[k, rows_, lanes] * ww[k, rows_, lanes] for k in range(8)]
        acc = car[0]
        for k in range(1, 8):
            acc = acc + car[k]
        m2[0, rows_, lanes] = acc
        for l in range(1, 9):
            acc = y_row(l, 0, it) * car[0]
            for k in range(1, 8):
                acc = acc + y_row(l, k, it) * car[k]
            m2[l, rows_, lanes] = acc

    @pl.loop(0, 2)
    def _(ch):
        sl = pl.ds(pl.multiple_of(ch * 256, 256), 256)
        q = [None, None, None]
        for l in range(9):
            m = m2[l, :, sl]
            g = 0 if l == 0 else (1 if l < 4 else 2)
            q[g] = m * m if q[g] is None else q[g] + m * m
        v = mixed(m2s, m2h, jnp.concatenate(q, 0))
        sg = 1.0 / (1.0 + jnp.exp(-v))
        dv = c_rd2 * (sg * (1.0 + v * (1.0 - sg)))
        dq = mixed(m2ts, m2th, dv) * 2.0
        for l in range(9):
            g = 0 if l == 0 else (1 if l < 4 else 2)
            m2[l, :, sl] = m2[l, :, sl] * dq[g * 128 : (g + 1) * 128]

    part[...] = jnp.zeros_like(part)

    @pl.loop(0, 16)
    def _(step):
        it = step // 4
        at = pl.multiple_of((step % 4) * 32, 32)
        rows_ = pl.ds(at, 32)
        rows_lo = pl.ds(at + 128, 32)
        lanes = pl.ds(pl.multiple_of(it * 128, 128), 128)
        dm = [m2[l, rows_, lanes] for l in range(9)]
        for k in range(8):
            g, w = gg[k, rows_, lanes], ww[k, rows_, lanes]
            car = g * w
            dcar = dm[0]
            for l in range(1, 9):
                dcar = dcar + y_row(l, k, it) * dm[l]
            for l in range(1, 9):
                pr = dm[l] * car
                pr = (pr[0:8] + pr[8:16]) + (pr[16:24] + pr[24:32])
                at8 = ((l - 1) * 8 + k) * 8
                part[at8 : at8 + 8, lanes] = part[at8 : at8 + 8, lanes] + pr
            edge = pl.ds(pl.multiple_of(k * 512 + it * 128, 128), 128)
            hi, lo = split(dcar * w)
            dg[rows_, edge] = hi
            dg[rows_lo, edge] = lo
            hi, lo = split(dcar * g)
            dw[rows_, edge] = hi
            dw[rows_lo, edge] = lo

    r2h, r2l = split(r2s)
    r2f = jnp.concatenate(
        [jnp.concatenate([r2h, r2h], 1).astype(F32), jnp.concatenate([r2l, jnp.zeros_like(r2l)], 1).astype(F32)], 0
    ).astype(BF16)
    for k in range(8):
        dbk = halves(dot(r2f, dw[:, k * 512 : (k + 1) * 512]))
        off, bk = basis(k)
        part[512 + k * 8 : 520 + k * 8, :] = -(dbk * bk * off)
    sel = (lax.broadcasted_iota(I32, (72, 576), 1) >> 3) == lax.broadcasted_iota(I32, (72, 576), 0)
    sel = jnp.where(sel, 1.0, 0.0).astype(BF16)
    ph, pl_ = split(part[...])
    two[...] = jnp.zeros_like(two)
    two[:, own_lanes] = dot(sel, ph) + dot(sel, pl_)

    @pl.loop(0, 4)
    def _(ch):
        at = pl.ds(pl.multiple_of(ch * 256, 256), 256)
        dh[:, at] = halves(dot_nt(dg[...], hot[at, :]))

    @pl.loop(0, 4)
    def _(ch):
        sl = pl.ds(pl.multiple_of(ch * 256, 256), 256)
        is_own = jnp.where(jnp.logical_or(ch == 1, ch == 2), 1.0, 0.0).astype(F32)
        dv = (dh[:, sl] + c_rd1 * is_own) * ds1[:, sl]
        dq = mixed(m1ts, m1th, dv) * 2.0
        on = geo[5, :, sl] > 0.5
        ux, uy, uz = geo[0, :, sl], geo[1, :, sl], geo[2, :, sl]
        s, inv = geo[3, :, sl], geo[4, :, sl]
        bs = [bb[n, :, sl] for n in range(8)]
        dy, db = [None], [None] * 8
        for l in range(9):
            g = 0 if l == 0 else (1 if l < 4 else 2)
            dm = m1[l, :, sl] * dq[g * 128 : (g + 1) * 128]
            dz = halves(dot(wtf, jnp.concatenate(split(dm), 0)))
            y = None if l == 0 else yy[l - 1, :, sl]
            acc = None
            for n in range(8):
                t = jnp.where(on, dz[64 + n * 8 : 72 + n * 8], dz[n * 8 : n * 8 + 8])
                if l == 0:
                    db[n] = t
                else:
                    db[n] = db[n] + t * y
                    acc = t * bs[n] if acc is None else acc + t * bs[n]
            if l:
                dy.append(acc + two[(l - 1) * 8 : l * 8, sl])
        dsv = two[64:72, sl]
        for n in range(8):
            dsv = dsv - db[n] * bs[n] * (s - (1.0 + n))
        dux = SQRT3 * dy[1] + SQRT15 * (uy * dy[4] + uz * dy[7] + ux * dy[8]) - SQRT5 * ux * dy[6]
        duy = SQRT3 * dy[2] + SQRT15 * (ux * dy[4] + uz * dy[5] - uy * dy[8]) - SQRT5 * uy * dy[6]
        duz = SQRT3 * dy[3] + SQRT15 * (uy * dy[5] + ux * dy[7]) + 2.0 * SQRT5 * uz * dy[6]
        along = dsv - (dux * ux + duy * uy + duz * uz) * inv
        dr[0, :, sl] = dux * inv + ux * along
        dr[1, :, sl] = duy * inv + uy * along
        dr[2, :, sl] = duz * inv + uz * along

    tile_ids = lax.broadcasted_iota(I32, (8, 1024), 0)
    lane_ids = lax.broadcasted_iota(I32, (128, 1024), 0)

    def onto(index_row, values):
        there = spread(index_row >> 7) == tile_ids
        his, los = [], []
        for v in values:
            m = jnp.where(there, spread(v), 0.0)
            hi = m.astype(BF16).astype(F32)
            his.append(hi)
            los.append(m - hi)
        lhs = jnp.concatenate(his + los, 0).astype(BF16)
        rhs = jnp.where(jnp.broadcast_to(index_row & 127, (128, 1024)) == lane_ids, 1.0, 0.0).astype(BF16)
        return lhs, rhs

    selfs = lax.broadcasted_iota(I32, (1, 1024), 1)
    lhs, rhs = onto(selfs, [-jnp.sum(dr[c], axis=0, keepdims=True) for c in range(3)])
    acc_own = dot_nt(lhs, rhs)
    acc_low = jnp.zeros((48, 128), F32)
    acc_up = jnp.zeros((48, 128), F32)
    for k in range(8):
        lhs, rhs = onto(nb_s[k : k + 1, :], [dr[c, k : k + 1, :] for c in range(3)])
        acc_own = acc_own + dot_nt(lhs[:, 256:768], rhs[:, 256:768])
        acc_low = acc_low + dot_nt(lhs[:, :256], rhs[:, :256])
        acc_up = acc_up + dot_nt(lhs[:, 768:], rhs[:, 768:])
    acc_own, acc_low, acc_up = halves(acc_own), halves(acc_low), halves(acc_up)

    def put(ref, at, acc, c, first, count):
        ref[at : at + count, :] = acc[c * 8 + first : c * 8 + first + count, :]

    for c in range(3):
        put(kept, c * 4, acc_own, c, 2, 4)
        put(kept, 12 + c * 4, acc_low, c, 6, 2)
        put(kept, 14 + c * 4, acc_up, c, 0, 2)
        put(to_low, c * 4, acc_low, c, 2, 4)
        put(to_low, 12 + c * 2, acc_own, c, 0, 2)
        put(to_up, c * 4, acc_up, c, 2, 4)
        put(to_up, 12 + c * 2, acc_own, c, 6, 2)
        put(to_low2, c * 2, acc_low, c, 0, 2)
        put(to_up2, c * 2, acc_up, c, 6, 2)
    pad2, pad6 = jnp.zeros((2, 128), F32), jnp.zeros((6, 128), F32)
    to_low[18:24, :] = pad6
    to_up[18:24, :] = pad6
    to_low2[6:8, :] = pad2
    to_up2[6:8, :] = pad2


COMPUTE_SCRATCH = [
    pltpu.VMEM((8, 1024), I32),
    pltpu.VMEM((6, 8, 1024), F32),
    pltpu.VMEM((8, 8, 1024), F32),
    pltpu.VMEM((8, 8, 1024), F32),
    pltpu.VMEM((1024, 4096), BF16),
    pltpu.VMEM((9, 128, 1024), F32),
    pltpu.VMEM((256, 1024), BF16),
    pltpu.VMEM((128, 1024), F32),
    pltpu.VMEM((8, 128, 512), F32),
    pltpu.VMEM((8, 128, 512), F32),
    pltpu.VMEM((9, 128, 512), F32),
    pltpu.VMEM((256, 4096), BF16),
    pltpu.VMEM((256, 4096), BF16),
    pltpu.VMEM((576, 512), F32),
    pltpu.VMEM((72, 1024), F32),
    pltpu.VMEM((128, 1024), F32),
    pltpu.VMEM((3, 8, 1024), F32),
    pltpu.VMEM((8, 1024), F32),
]


def compute(own, low1, up1, low2, up2, emb, r1, r2, mix1, mix2, rd1, rd2):
    shape = lambda n: jax.ShapeDtypeStruct((n, 128), F32)
    return pl.pallas_call(
        compute_kernel,
        out_shape=(shape(24), shape(24), shape(8), shape(8), shape(24)),
        in_specs=[VM] * 12,
        out_specs=(VM,) * 5,
        scratch_shapes=COMPUTE_SCRATCH,
        compiler_params=pltpu.CompilerParams(vmem_limit_bytes=60 << 20),
        name="energy_gradient",
    )(own, low1, up1, low2, up2, emb, r1, r2, mix1, mix2, rd1, rd2)


def halo_kernel(domains, mine, low1, up1, low2, up2, send_sem, recv_sem):
    me = lax.axis_index("space")
    peers = [lax.rem(me + s + domains, domains) for s in (1, -1, 2, -2)]
    barrier = pltpu.get_barrier_semaphore()
    for p in peers:
        pl.semaphore_signal(barrier, inc=1, device_id={"space": p}, device_id_type=MESH)
    pl.semaphore_wait(barrier, 4)
    src = (mine, mine, mine.at[0:8], mine.at[0:8])
    copies = []
    for i, (p, s, dst) in enumerate(zip(peers, src, (low1, up1, low2, up2))):
        copies.append(
            pltpu.make_async_remote_copy(
                src_ref=s, dst_ref=dst, send_sem=send_sem.at[i], recv_sem=recv_sem.at[i],
                device_id={"space": p}, device_id_type=MESH,
            )
        )
        copies[-1].start()
    for c in copies:
        c.wait()


def halo(mine, domains):
    shape = lambda n: jax.ShapeDtypeStruct((n, 512), F32)
    return pl.pallas_call(
        lambda *refs: halo_kernel(domains, *refs),
        out_shape=(shape(16), shape(16), shape(8), shape(8)),
        in_specs=[VM],
        out_specs=(VM,) * 4,
        scratch_shapes=[pltpu.SemaphoreType.DMA((4,)), pltpu.SemaphoreType.DMA((4,))],
        compiler_params=pltpu.CompilerParams(collective_id=0, has_side_effects=True),
        name="halo",
    )(mine)


def ring_tables(beads):
    b = np.arange(beads, dtype=np.float64)
    angle = beads * np.sin(np.pi * b / beads)
    safe = np.where(b == 0, 1.0, angle)
    reach = np.where(b == 0, STEP, STEP * np.sin(angle) / safe)
    stiff = angle * np.sin(angle) / STEP
    phase = np.cos(2.0 * np.pi * np.outer(b, b) / beads) / beads
    return [(phase @ f).tolist() for f in (np.cos(angle), reach, stiff)]


def rows12(ref):
    return jnp.concatenate([ref[c : c + 1, t * 128 : (t + 1) * 128] for c in range(3) for t in range(4)], 0)


def finish_kernel(
    domains, beads,
    to_low, to_up, to_low2, to_up2, kept, pos, mom, mine,
    new_pos, new_mom,
    from_low, from_up, from_low2, from_up2, q_src, p_src, q_all, p_all,
    hs_sem, hr_sem, qs_sem, qr_sem, ps_sem, pr_sem,
):
    me = lax.axis_index("space")
    bead = lax.axis_index("bead")
    near = [lax.rem(me + s + domains, domains) for s in (1, -1, 2, -2)]
    ring = [lax.rem(bead + o, beads) for o in range(beads)]
    barrier = pltpu.get_barrier_semaphore()
    for p in near:
        pl.semaphore_signal(barrier, inc=1, device_id={"space": p}, device_id_type=MESH)
    for o in range(1, beads):
        pl.semaphore_signal(barrier, inc=1, device_id={"bead": ring[o]}, device_id_type=MESH)
    q_src[...] = rows12(pos)
    pl.semaphore_wait(barrier, 4 + beads - 1)

    copies = []
    for i, (p, s, dst) in enumerate(
        zip(near, (to_up, to_low, to_up2, to_low2), (from_low, from_up, from_low2, from_up2))
    ):
        copies.append(
            pltpu.make_async_remote_copy(
                src_ref=s, dst_ref=dst, send_sem=hs_sem.at[i], recv_sem=hr_sem.at[i],
                device_id={"space": p}, device_id_type=MESH,
            )
        )
        copies[-1].start()

    def share(src, dst, s_sem, r_sem):
        out = []
        for o in range(1, beads):
            c = pltpu.make_async_remote_copy(
                src_ref=src, dst_ref=dst.at[o], send_sem=s_sem.at[o], recv_sem=r_sem.at[o],
                device_id={"bead": ring[o]}, device_id_type=MESH,
            )
            c.start()
            out.append(c)
        return out

    q_copies = share(q_src, q_all, qs_sem, qr_sem)
    send = mine[4:5, :].astype(I32)
    there = [spread(send[:, t * 128 : (t + 1) * 128] >> 7) for t in range(4)]
    iota8 = lax.broadcasted_iota(I32, (8, 128), 0)
    rhs = jnp.where(
        jnp.broadcast_to(send & 127, (128, 512)) == lax.broadcasted_iota(I32, (128, 512), 0), 1.0, 0.0
    ).astype(BF16)
    mass4 = HEAVY - (HEAVY - 1.0) * jnp.concatenate(
        [mine[3:4, t * 128 : (t + 1) * 128] for t in range(4)], 0
    )
    mass = jnp.concatenate([mass4, mass4, mass4], 0)
    p12 = rows12(mom)
    for c in copies:
        c.wait()

    his, los = [], []
    for c in range(3):
        parts = []
        for t in range(4):
            near_, far = (from_low, from_low2) if t < 2 else (from_up, from_up2)
            at, a12, a2 = 12 + c * 4 + t, 12 + c * 2 + t % 2, c * 2 + t % 2
            v = kept[at : at + 1, :] + near_[a12 : a12 + 1, :] + far[a2 : a2 + 1, :]
            parts.append(jnp.where(there[t] == iota8, spread(v), 0.0))
        m = jnp.concatenate(parts, 1)
        hi = m.astype(BF16).astype(F32)
        his.append(hi)
        los.append(m - hi)
    got = halves(dot_nt(jnp.concatenate(his + los, 0).astype(BF16), rhs))
    got = jnp.concatenate([got[c * 8 : c * 8 + 4] for c in range(3)], 0)
    kicked = p12 - (kept[0:12, :] + from_low[0:12, :] + from_up[0:12, :] + got)
    p_src[...] = kicked
    p_copies = share(p_src, p_all, ps_sem, pr_sem)

    turn, reach, stiff = ring_tables(beads)
    q = q_src[...]
    qa, qs = turn[0] * q, stiff[0] * q
    for o, c in zip(range(1, beads), q_copies):
        c.wait()
        q = q_all[o]
        qa, qs = qa + turn[o] * q, qs + stiff[o] * q
    pa, pr = turn[0] * kicked, reach[0] * kicked
    for o, c in zip(range(1, beads), p_copies):
        c.wait()
        p = p_all[o]
        pa, pr = pa + turn[o] * p, pr + reach[o] * p
    qn = qa + pr / mass
    pn = pa - mass * qs
    for c in range(3):
        for t in range(4):
            at = c * 4 + t
            new_pos[c : c + 1, t * 128 : (t + 1) * 128] = qn[at : at + 1]
            new_mom[c : c + 1, t * 128 : (t + 1) * 128] = pn[at : at + 1]


def finish(pieces, pos, mom, mine, domains, beads):
    dma = lambda n: pltpu.SemaphoreType.DMA((n,))
    return pl.pallas_call(
        lambda *refs: finish_kernel(domains, beads, *refs),
        out_shape=(jax.ShapeDtypeStruct((3, 512), F32),) * 2,
        in_specs=[VM] * 8,
        out_specs=(VM,) * 2,
        scratch_shapes=[
            pltpu.VMEM((24, 128), F32), pltpu.VMEM((24, 128), F32),
            pltpu.VMEM((8, 128), F32), pltpu.VMEM((8, 128), F32),
            pltpu.VMEM((12, 128), F32), pltpu.VMEM((12, 128), F32),
            pltpu.VMEM((beads, 12, 128), F32), pltpu.VMEM((beads, 12, 128), F32),
            dma(4), dma(4), dma(beads), dma(beads), dma(beads), dma(beads),
        ],
        compiler_params=pltpu.CompilerParams(collective_id=1, has_side_effects=True),
        name="finish",
    )(*pieces, pos, mom, mine)


def shards(
    positions, momenta, species, neighbours, send_list, embedding,
    radial_one, radial_two, mix_one, mix_two, read_one, read_two,
):
    domains, beads = lax.axis_size("space"), lax.axis_size("bead")
    mine = jnp.concatenate(
        [
            positions[0], species.astype(F32)[None], send_list.astype(F32)[None],
            jnp.zeros((3, 512), F32), neighbours.astype(F32),
        ],
        0,
    )
    near = halo(mine, domains)
    pieces = compute(
        mine, *near, embedding, radial_one, radial_two, mix_one, mix_two, read_one[None], read_two[None]
    )
    q, p = finish(pieces, positions[0], momenta[0], mine, domains, beads)
    return q[None], p[None]


def solution(mesh):
    beads = P("bead", None, "space")
    placed = (beads, beads, P("space"), P(None, "space"), P("space")) + (P(),) * 7
    return jax.shard_map(shards, mesh=mesh, in_specs=placed, out_specs=(beads, beads), check_vma=False)
```

time: 335 us -> 71.4 us (0.21); the launches traced: 329 us -> 71 us
  other arithmetic: 95.8 us -> 0.75 us
  matrix products: 78.6 us -> 0 us
  local copies, waits for them, and re-layouts: 72.6 us -> 5.1 us
  Pallas kernels: 0 us -> 64.5 us
  waiting for transfers between devices: 45.7 us -> 0 us
  starting transfers between devices: 34.3 us -> 0 us
    dot_general x21 -> x0, matrix products: 78.6 us -> none  [the longest x6 53.6 us: interaction(): jnp.einsum('lka,cka->lca', sphere, carried, precision=EXACT) / neigh_count]
    scatter-add x5 -> x0, other arithmetic: 76 us -> none  [the longest x2 45.4 us: interaction(): jnp.take(ext_coords, flat_slots, axis=1).reshape(3, neigh_count, atom_count)]
    pallas_call x0 -> x3, Pallas kernels: none -> 64.5 us  [the longest x1 27 us: compute(): pl.pallas_call(compute_kernel, out_shape=(shape(24), shape(24), shape(8),...]
    gather x6 -> x0, local copies, waits for them, and re-layouts: 44.8 us -> none  [the longest x2 28.4 us: interaction(): jnp.take(ext_feat, flat_slots, axis=1).reshape(-1, neigh_count, atom_count)]
    ppermute x8 -> x0, waiting for transfers between devices: 32.9 us -> none  [the longest x4 28.6 us: padded(): lax.ppermute(tail, axis, [(i, (i + 1) % count) for i in range(count)])]
    ppermute x8 -> x0, starting transfers between devices: 26.7 us -> none  [the longest x4 16.5 us: padded(): lax.ppermute(head, axis, [((i + 1) % count, i) for i in range(count)])]
    all_to_all x1 -> x0, waiting for transfers between devices: 12.8 us -> none  [sent_to_all(): return lax.all_to_all(copies, axis, split_axis=0, concat_axis=0, tiled=True)]
    all_to_all x1 -> x0, starting transfers between devices: 7.64 us -> none  [sent_to_all(): return lax.all_to_all(copies, axis, split_axis=0, concat_axis=0, tiled=True)]
  transfers between devices with their start and end apart: 9 -> 0, of which waited for: 8 -> 0; matrix products, arithmetic and copies ran while one was open for 4% -> 0% of each run, Pallas kernels for 0% -> 0%
where the time goes in v1:
time: 71.4 us; the launch traced here: 71 us
  Pallas kernels  64.5 us (90%)
  local copies, waits for them, and re-layouts  5.1 us (7%)
  other arithmetic  0.75 us (1%)
    pallas_call x1, Pallas kernels, compute(): pl.pallas_call(compute_kernel, out_shape=(shape(24), shape(24), shape(8),...  27 us
    pallas_call x1, Pallas kernels, finish(): pl.pallas_call(lambda *refs: finish_kernel(domains, beads, *refs), out_sh...  23.7 us
    pallas_call x1, Pallas kernels, halo(): pl.pallas_call(lambda *refs: halo_kernel(domains, *refs), out_shape=(shap...  13.9 us
    unnamed x15, local copies, waits for them, and re-layouts  3.87 us

profile of v1, /device:TPU:1, one launch (start us, length us, event | category | flops | bytes accessed | tf_op | source)
XLA Modules:
  0.0 71.0 jit_solution(16179599469029530052)
XLA Ops:
  0.6 0.0 copy-start.4
  0.6 0.7 copy-done.4
  1.3 0.0 copy-start.5
  1.3 0.7 copy-done.5
  2.0 0.0 copy-start.2
  2.0 0.0 copy-start.3
  2.0 0.7 %convert_element_type.11 = f32[8,512]{1,0:T(8,128)S(1)} convert(s32[8,512]{1,0:T(8,128)} %param.15) | non-fusion elementwise | flops 4096 | bytes 32768 | tf_op jit(solution)/shard_map/convert_element_type | solution.py:560
  2.7 0.0 copy-done.2
  2.8 0.0 copy-done.3
  2.8 0.6 copy_bitcast_fusion
  3.4 0.0 copy-start
  3.4 1.2 %concatenate.3.refs_0_.own.refs_7_ = f32[16,512]{1,0:T(8,128)} concatenate(f32[3,512]{1,0:T(4,128)S(1)} %get-tuple-element.27.refs_5_, f32[1,512]{1,0:T(1,128)S(1)} %bitcast.12, f32[1,512]{1,0:T(1,128)S(1)} %bitcast.13, f32[3,512]{1,0:T(4,128)S(1)} %broadcast_in_dim.23, f32[8,512]{1,0:T(8,128)S(1)} %convert_element_type.11), dimensions={0} | concatenate | bytes 65536 | tf_op jit(solution)/shard_map/concatenate | solution.py:557
  4.6 0.0 copy-done
  4.6 13.9 %halo.1 = (f32[16,512]{1,0:T(8,128)}, f32[16,512]{1,0:T(8,128)}, f32[8,512]{1,0:T(8,128)}, f32[8,512]{1,0:T(8,128)}) custom-call(f32[16,512]{1,0:T(8,128)} %concatenate.3.refs_0_.own.refs_7_), custom_call_target="tpu_custom_call" | custom-call | tf_op jit(solution)/shard_map/halo/pallas_call | solution.py:412
  18.5 27.0 %energy_gradient.1 = (f32[24,128]{1,0:T(8,128)}, f32[24,128]{1,0:T(8,128)}, f32[8,128]{1,0:T(8,128)}, f32[8,128]{1,0:T(8,128)}, f32[24,128]{1,0:T(8,128)}) custom-call(f32[16,512]{1,0:T(8,128)} %concatenate.3.refs_0_.own.refs_7_, f32[16,512]{1,0:T(8,128)} %get-tuple-element.13.low1, f32[16,512]{1,0:T(8,128)} %get-tuple-element.14.up1, ...), custom_call_target="tpu_custom_call" | custom-call | tf_op jit(solution)/shard_map/energy_gradient/pallas_call | solution.py:378
  45.4 23.7 %finish.1 = (f32[3,512]{1,0:T(4,128)}, f32[3,512]{1,0:T(4,128)}) custom-call(f32[24,128]{1,0:T(8,128)} %get-tuple-element.17.refs_0_, f32[24,128]{1,0:T(8,128)} %get-tuple-element.18.refs_1_, f32[8,128]{1,0:T(8,128)} %get-tuple-element.19.refs_2_, f32[8,128]{1,0:T(8,128)} %get-tuple-element.20.refs_3_, f32[24,128]{1,0:T(8,128)} %get-tuple-element.21.refs_4_, ...), custom_call_target="tpu_custom_call" | custom-call | tf_op jit(solution)/shard_map/finish/pallas_call | solution.py:535
  69.1 0.0 copy-start.1
  69.1 1.3 %copy.14 = f32[1,3,512]{2,0,1:T(1,128)} copy(f32[1,3,512]{2,1,0:T(4,128)} %bitcast.11) | data formatting | bytes 12288
  70.4 0.0 copy-done.1
  70.4 0.6 copy.15
  (3 shorter events, 0.0 us)
Async XLA Ops:
  0.6 0.7 copy-start.4
  1.3 0.7 copy-start.5
  2.0 0.8 %copy-start.2 = (f32[1,3,512]{2,0,1:T(1,128)S(1)}, f32[1,3,512]{2,0,1:T(1,128)}, u32[]{:S(2)}) copy-start(f32[1,3,512]{2,0,1:T(1,128)} %param.13) | copy-start | bytes 18436
  2.0 0.8 %copy-start.3 = (f32[1,3,512]{2,0,1:T(1,128)S(1)}, f32[1,3,512]{2,0,1:T(1,128)}, u32[]{:S(2)}) copy-start(f32[1,3,512]{2,0,1:T(1,128)} %param.12) | copy-start | bytes 18436
  3.4 1.2 %copy-start = (f32[3,512]{1,0:T(4,128)}, f32[3,512]{1,0:T(4,128)S(1)}, u32[]{:S(2)}) copy-start(f32[3,512]{1,0:T(4,128)S(1)} %get-tuple-element.27.refs_5_) | copy-start | bytes 18436
  69.1 1.3 %copy-start.1 = (f32[3,512]{1,0:T(4,128)S(1)}, f32[3,512]{1,0:T(4,128)}, u32[]{:S(2)}) copy-start(f32[3,512]{1,0:T(4,128)} %get-tuple-element.23) | copy-start | bytes 18436

commit v2 on v1

--- a/solution.py
+++ b/solution.py
@@ -54,35 +54,21 @@
     return jnp.broadcast_to(row, (count, row.shape[1]))
 
 
-def tiles_of(ref, first):
-    return [ref[first : first + 8, t * 128 : (t + 1) * 128] for t in range(4)]
-
-
-def compute_kernel(
-    own, low1, up1, low2, up2, emb, r1, r2, mix1, mix2, rd1, rd2,
+def build_hot(nbr, hot):
+    @pl.loop(0, 8)
+    def _(rc):
+        at = pl.multiple_of(rc * 128, 128)
+        ids = lax.broadcasted_iota(I32, (128, 512), 0) + at
+        for k in range(8):
+            row = jnp.broadcast_to(nbr[k : k + 1, :], (128, 512))
+            hot[pl.ds(at, 128), k * 512 : (k + 1) * 512] = jnp.where(ids == row, 1.0, 0.0).astype(BF16)
+
+
+def energy_gradient(
+    ext_own, ext_low, ext_up, nb_t, emb, r1, r2, mix1, mix2, rd1, rd2,
     to_low, to_up, to_low2, to_up2, kept,
     nb_s, geo, yy, bb, hot, m1, hs, ds1, gg, ww, m2, dg, dw, part, two, dh, dr, fl,
 ):
-    def send_of(ref):
-        return ref[4:5, :].astype(I32)
-
-    sends = [send_of(r) for r in (own, low1, up1, low2, up2)]
-
-    def slots(ref, send, half, first=0):
-        tiles = tiles_of(ref, first)
-        out = []
-        for t in range(2):
-            at = half * 256 + t * 128
-            out.append(lane_take(tiles, spread(send[:, at : at + 128])))
-        return out
-
-    own_t = tiles_of(own, 0)
-    ext_own = slots(low1, sends[1], 1) + own_t + slots(up1, sends[2], 0)
-    ext_low = slots(low2, sends[3], 1) + tiles_of(low1, 0) + slots(own, sends[0], 0)
-    ext_up = slots(own, sends[0], 1) + tiles_of(up1, 0) + slots(up2, sends[4], 0)
-    nb_t = slots(low1, sends[1], 1, 8) + tiles_of(own, 8) + slots(up1, sends[2], 0, 8)
-    nb_t = [x.astype(I32) for x in nb_t]
-
     for e in range(8):
         cols = slice(e * 128, (e + 1) * 128)
         ext = ext_low if e < 2 else (ext_own if e < 6 else ext_up)
@@ -106,14 +92,6 @@
             yy[l, :, cols] = ys[l]
         for n in range(8):
             bb[n, :, cols] = jnp.exp(-0.5 * (s - (1.0 + n)) ** 2)
-
-    @pl.loop(0, 8)
-    def _(rc):
-        at = pl.multiple_of(rc * 128, 128)
-        ids = lax.broadcasted_iota(I32, (128, 512), 0) + at
-        for k in range(8):
-            row = jnp.broadcast_to(nb_s[k : k + 1, 256:768], (128, 512))
-            hot[pl.ds(at, 128), k * 512 : (k + 1) * 512] = jnp.where(ids == row, 1.0, 0.0).astype(BF16)
 
     w_rows = []
     for f in range(2):
@@ -373,53 +351,6 @@
 ]
 
 
-def compute(own, low1, up1, low2, up2, emb, r1, r2, mix1, mix2, rd1, rd2):
-    shape = lambda n: jax.ShapeDtypeStruct((n, 128), F32)
-    return pl.pallas_call(
-        compute_kernel,
-        out_shape=(shape(24), shape(24), shape(8), shape(8), shape(24)),
-        in_specs=[VM] * 12,
-        out_specs=(VM,) * 5,
-        scratch_shapes=COMPUTE_SCRATCH,
-        compiler_params=pltpu.CompilerParams(vmem_limit_bytes=60 << 20),
-        name="energy_gradient",
-    )(own, low1, up1, low2, up2, emb, r1, r2, mix1, mix2, rd1, rd2)
-
-
-def halo_kernel(domains, mine, low1, up1, low2, up2, send_sem, recv_sem):
-    me = lax.axis_index("space")
-    peers = [lax.rem(me + s + domains, domains) for s in (1, -1, 2, -2)]
-    barrier = pltpu.get_barrier_semaphore()
-    for p in peers:
-        pl.semaphore_signal(barrier, inc=1, device_id={"space": p}, device_id_type=MESH)
-    pl.semaphore_wait(barrier, 4)
-    src = (mine, mine, mine.at[0:8], mine.at[0:8])
-    copies = []
-    for i, (p, s, dst) in enumerate(zip(peers, src, (low1, up1, low2, up2))):
-        copies.append(
-            pltpu.make_async_remote_copy(
-                src_ref=s, dst_ref=dst, send_sem=send_sem.at[i], recv_sem=recv_sem.at[i],
-                device_id={"space": p}, device_id_type=MESH,
-            )
-        )
-        copies[-1].start()
-    for c in copies:
-        c.wait()
-
-
-def halo(mine, domains):
-    shape = lambda n: jax.ShapeDtypeStruct((n, 512), F32)
-    return pl.pallas_call(
-        lambda *refs: halo_kernel(domains, *refs),
-        out_shape=(shape(16), shape(16), shape(8), shape(8)),
-        in_specs=[VM],
-        out_specs=(VM,) * 4,
-        scratch_shapes=[pltpu.SemaphoreType.DMA((4,)), pltpu.SemaphoreType.DMA((4,))],
-        compiler_params=pltpu.CompilerParams(collective_id=0, has_side_effects=True),
-        name="halo",
-    )(mine)
-
-
 def ring_tables(beads):
     b = np.arange(beads, dtype=np.float64)
     angle = beads * np.sin(np.pi * b / beads)
@@ -431,15 +362,18 @@
 
 
 def rows12(ref):
-    return jnp.concatenate([ref[c : c + 1, t * 128 : (t + 1) * 128] for c in range(3) for t in range(4)], 0)
-
-
-def finish_kernel(
+    return jnp.concatenate([ref[c, 0:1, t * 128 : (t + 1) * 128] for c in range(3) for t in range(4)], 0)
+
+
+def step_kernel(
     domains, beads,
-    to_low, to_up, to_low2, to_up2, kept, pos, mom, mine,
+    pos, mom, spec, nbr, send_ref, emb, r1, r2, mix1, mix2, rd1, rd2,
     new_pos, new_mom,
+    msg_up, msg_low, in_low, in_up, in_low2, in_up2,
+    to_low, to_up, to_low2, to_up2, kept,
     from_low, from_up, from_low2, from_up2, q_src, p_src, q_all, p_all,
-    hs_sem, hr_sem, qs_sem, qr_sem, ps_sem, pr_sem,
+    fs_sem, fr_sem, hs_sem, hr_sem, qs_sem, qr_sem, ps_sem, pr_sem,
+    *work,
 ):
     me = lax.axis_index("space")
     bead = lax.axis_index("bead")
@@ -450,20 +384,48 @@
         pl.semaphore_signal(barrier, inc=1, device_id={"space": p}, device_id_type=MESH)
     for o in range(1, beads):
         pl.semaphore_signal(barrier, inc=1, device_id={"bead": ring[o]}, device_id_type=MESH)
+
+    flags = spec[...].astype(F32)
+    send = send_ref[...]
+    own_t, nbr_t = [], []
+    for t in range(4):
+        lanes = slice(t * 128, (t + 1) * 128)
+        quad = [pos[c, 0:1, lanes] for c in range(3)] + [flags[:, lanes]]
+        own_t.append(jnp.concatenate(quad + quad, 0))
+        nbr_t.append(nbr[:, lanes])
+
+    def sent(tiles, half):
+        return [
+            lane_take(tiles, spread(send[:, at : at + 128])) for at in (half * 256, half * 256 + 128)
+        ]
+
+    def pair(x, y):
+        return jnp.concatenate([x[0:4], y[4:8]], 0)
+
+    def both(x):
+        return [jnp.concatenate([x[0:4], x[0:4]], 0), jnp.concatenate([x[4:8], x[4:8]], 0)]
+
+    ghosts = [sent(own_t, 0), sent(own_t, 1)]
     q_src[...] = rows12(pos)
+    for msg, half in ((msg_low, 0), (msg_up, 1)):
+        lists = sent(nbr_t, half)
+        msg[0:8, :] = pair(own_t[0], own_t[1])
+        msg[8:16, :] = pair(own_t[2], own_t[3])
+        msg[16:24, :] = pair(*ghosts[half])
+        msg[24:32, :] = lists[0].astype(F32)
+        msg[32:40, :] = lists[1].astype(F32)
     pl.semaphore_wait(barrier, 4 + beads - 1)
 
-    copies = []
-    for i, (p, s, dst) in enumerate(
-        zip(near, (to_up, to_low, to_up2, to_low2), (from_low, from_up, from_low2, from_up2))
-    ):
-        copies.append(
-            pltpu.make_async_remote_copy(
-                src_ref=s, dst_ref=dst, send_sem=hs_sem.at[i], recv_sem=hr_sem.at[i],
+    def to_near(srcs, dsts, s_sem, r_sem):
+        out = []
+        for i, (p, s, dst) in enumerate(zip(near, srcs, dsts)):
+            c = pltpu.make_async_remote_copy(
+                src_ref=s, dst_ref=dst, send_sem=s_sem.at[i], recv_sem=r_sem.at[i],
                 device_id={"space": p}, device_id_type=MESH,
             )
-        )
-        copies[-1].start()
+            c.start()
+            out.append(c)
+        return out
 
     def share(src, dst, s_sem, r_sem):
         out = []
@@ -476,15 +438,37 @@
             out.append(c)
         return out
 
+    halo = to_near(
+        (msg_up, msg_low, msg_up.at[16:24], msg_low.at[16:24]), (in_low, in_up, in_low2, in_up2), fs_sem, fr_sem
+    )
+    build_hot(nbr, work[4])
+    for c in halo:
+        c.wait()
     q_copies = share(q_src, q_all, qs_sem, qr_sem)
-    send = mine[4:5, :].astype(I32)
+
+    def whole(ref):
+        return both(ref[0:8, :]) + both(ref[8:16, :])
+
+    ext_own = both(in_low[16:24, :]) + own_t + both(in_up[16:24, :])
+    ext_low = both(in_low2[...]) + whole(in_low) + ghosts[0]
+    ext_up = ghosts[1] + whole(in_up) + both(in_up2[...])
+    nb_t = [in_low[24:32, :].astype(I32), in_low[32:40, :].astype(I32)] + nbr_t
+    nb_t = nb_t + [in_up[24:32, :].astype(I32), in_up[32:40, :].astype(I32)]
+    energy_gradient(
+        ext_own, ext_low, ext_up, nb_t, emb, r1, r2, mix1, mix2, rd1, rd2,
+        to_low, to_up, to_low2, to_up2, kept, *work,
+    )
+    copies = to_near(
+        (to_up, to_low, to_up2, to_low2), (from_low, from_up, from_low2, from_up2), hs_sem, hr_sem
+    )
+
     there = [spread(send[:, t * 128 : (t + 1) * 128] >> 7) for t in range(4)]
     iota8 = lax.broadcasted_iota(I32, (8, 128), 0)
     rhs = jnp.where(
         jnp.broadcast_to(send & 127, (128, 512)) == lax.broadcasted_iota(I32, (128, 512), 0), 1.0, 0.0
     ).astype(BF16)
     mass4 = HEAVY - (HEAVY - 1.0) * jnp.concatenate(
-        [mine[3:4, t * 128 : (t + 1) * 128] for t in range(4)], 0
+        [flags[:, t * 128 : (t + 1) * 128] for t in range(4)], 0
     )
     mass = jnp.concatenate([mass4, mass4, mass4], 0)
     p12 = rows12(mom)
@@ -526,27 +510,8 @@
     for c in range(3):
         for t in range(4):
             at = c * 4 + t
-            new_pos[c : c + 1, t * 128 : (t + 1) * 128] = qn[at : at + 1]
-            new_mom[c : c + 1, t * 128 : (t + 1) * 128] = pn[at : at + 1]
-
-
-def finish(pieces, pos, mom, mine, domains, beads):
-    dma = lambda n: pltpu.SemaphoreType.DMA((n,))
-    return pl.pallas_call(
-        lambda *refs: finish_kernel(domains, beads, *refs),
-        out_shape=(jax.ShapeDtypeStruct((3, 512), F32),) * 2,
-        in_specs=[VM] * 8,
-        out_specs=(VM,) * 2,
-        scratch_shapes=[
-            pltpu.VMEM((24, 128), F32), pltpu.VMEM((24, 128), F32),
-            pltpu.VMEM((8, 128), F32), pltpu.VMEM((8, 128), F32),
-            pltpu.VMEM((12, 128), F32), pltpu.VMEM((12, 128), F32),
-            pltpu.VMEM((beads, 12, 128), F32), pltpu.VMEM((beads, 12, 128), F32),
-            dma(4), dma(4), dma(beads), dma(beads), dma(beads), dma(beads),
-        ],
-        compiler_params=pltpu.CompilerParams(collective_id=1, has_side_effects=True),
-        name="finish",
-    )(*pieces, pos, mom, mine)
+            new_pos[c, 0:1, t * 128 : (t + 1) * 128] = qn[at : at + 1]
+            new_mom[c, 0:1, t * 128 : (t + 1) * 128] = pn[at : at + 1]
 
 
 def shards(
@@ -554,19 +519,25 @@
     radial_one, radial_two, mix_one, mix_two, read_one, read_two,
 ):
     domains, beads = lax.axis_size("space"), lax.axis_size("bead")
-    mine = jnp.concatenate(
-        [
-            positions[0], species.astype(F32)[None], send_list.astype(F32)[None],
-            jnp.zeros((3, 512), F32), neighbours.astype(F32),
-        ],
-        0,
+    dma = lambda n: pltpu.SemaphoreType.DMA((n,))
+    rows = lambda n: pltpu.VMEM((n, 128), F32)
+    q, p = pl.pallas_call(
+        lambda *refs: step_kernel(domains, beads, *refs),
+        out_shape=(jax.ShapeDtypeStruct((3, 1, 512), F32),) * 2,
+        in_specs=[VM] * 12,
+        out_specs=(VM,) * 2,
+        scratch_shapes=[rows(n) for n in (40, 40, 40, 40, 8, 8, 24, 24, 8, 8, 24, 24, 24, 8, 8, 12, 12)]
+        + [pltpu.VMEM((beads, 12, 128), F32)] * 2
+        + [dma(4)] * 4 + [dma(beads)] * 4 + COMPUTE_SCRATCH,
+        compiler_params=pltpu.CompilerParams(
+            collective_id=0, has_side_effects=True, vmem_limit_bytes=60 << 20
+        ),
+        name="md_step",
+    )(
+        jnp.transpose(positions, (1, 0, 2)), jnp.transpose(momenta, (1, 0, 2)), species[None], neighbours,
+        send_list[None], embedding, radial_one, radial_two, mix_one, mix_two, read_one[None], read_two[None],
     )
-    near = halo(mine, domains)
-    pieces = compute(
-        mine, *near, embedding, radial_one, radial_two, mix_one, mix_two, read_one[None], read_two[None]
-    )
-    q, p = finish(pieces, positions[0], momenta[0], mine, domains, beads)
-    return q[None], p[None]
+    return jnp.transpose(q, (1, 0, 2)), jnp.transpose(p, (1, 0, 2))
 
 
 def solution(mesh):

time: 71.4 us -> 59.1 us (0.83)
  Pallas kernels: 64.5 us -> 56.3 us
  local copies, waits for them, and re-layouts: 5.1 us -> 1.97 us
  other arithmetic: 0.75 us -> 0 us
    pallas_call x3 -> x1, Pallas kernels: 64.5 us -> 56.3 us  [shards(): pl.pallas_call(lambda *refs: step_kernel(domains, beads, *refs), out_shap...]
    unnamed x15 -> x6, local copies, waits for them, and re-layouts: 3.87 us -> 1.97 us
    concatenate x1 -> x0, local copies, waits for them, and re-layouts: 1.23 us -> none  [shards(): jnp.concatenate([positions[0], species.astype(F32)[None], send_list.astyp...]
    convert_element_type x3 -> x0, other arithmetic: 0.75 us -> none  [the longest x1 0.75 us: shards(): neighbours.astype(F32)]
where the time goes in v2:
time: 59.1 us; the launch traced here: 58.9 us
  Pallas kernels  56.3 us (95%)
  local copies, waits for them, and re-layouts  1.97 us (3%)
  between operations  0.65 us (1%)
    pallas_call x1, Pallas kernels, shards(): pl.pallas_call(lambda *refs: step_kernel(domains, beads, *refs), out_shap...  56.3 us
    unnamed x6, local copies, waits for them, and re-layouts  1.97 us

profile of v2, /device:TPU:1, one launch (start us, length us, event | category | flops | bytes accessed | tf_op | source)
XLA Modules:
  0.0 58.9 jit_solution(11027292101938555774)
XLA Ops:
  0.6 56.3 %md_step.1 = (f32[3,1,512]{2,1,0:T(1,128)}, f32[3,1,512]{2,1,0:T(1,128)}) custom-call(f32[3,1,512]{2,1,0:T(1,128)} %bitcast.10, f32[3,1,512]{2,1,0:T(1,128)} %bitcast.11, s32[1,512]{1,0:T(1,128)} %bitcast.12, s32[8,512]{1,0:T(8,128)} %refs_3_.1, s32[1,512]{1,0:T(1,128)} %bitcast.13, f32[2,128]{1,0:T(2,128)} %refs_5_.1, f32[8,128]{1,0:T(8,128)} %refs_6_.1, ...), custom_call_target="tpu_custom_call" | custom-call | tf_op jit(solution)/shard_map/md_step/pallas_call | solution.py:524
  56.9 0.0 copy-start.1
  56.9 0.7 %copy-done.1 = f32[3,1,512]{2,1,0:T(1,128)S(1)} copy-done((f32[3,1,512]{2,1,0:T(1,128)S(1)}, f32[3,1,512]{2,1,0:T(1,128)}, u32[]{:S(2)}) %copy-start.1) | copy-done | bytes 6168
  57.6 0.0 copy-start
  57.6 0.6 %copy.16 = f32[1,3,512]{2,0,1:T(1,128)} copy(f32[1,3,512]{2,0,1:T(1,128)S(1)} %bitcast.9) | data formatting | bytes 12288
  58.2 0.1 copy-done
  58.3 0.6 %copy.17 = f32[1,3,512]{2,0,1:T(1,128)} copy(f32[1,3,512]{2,0,1:T(1,128)S(1)} %bitcast.8) | data formatting | bytes 12288
Async XLA Ops:
  56.9 0.7 %copy-start.1 = (f32[3,1,512]{2,1,0:T(1,128)S(1)}, f32[3,1,512]{2,1,0:T(1,128)}, u32[]{:S(2)}) copy-start(f32[3,1,512]{2,1,0:T(1,128)} %get-tuple-element.4) | copy-start | bytes 18436
  57.6 0.7 %copy-start = (f32[3,1,512]{2,1,0:T(1,128)S(1)}, f32[3,1,512]{2,1,0:T(1,128)}, u32[]{:S(2)}) copy-start(f32[3,1,512]{2,1,0:T(1,128)} %get-tuple-element.5) | copy-start | bytes 18436

commit v3 on v2

--- a/solution.py
+++ b/solution.py
@@ -58,14 +58,15 @@
     @pl.loop(0, 8)
     def _(rc):
         at = pl.multiple_of(rc * 128, 128)
-        ids = lax.broadcasted_iota(I32, (128, 512), 0) + at
-        for k in range(8):
-            row = jnp.broadcast_to(nbr[k : k + 1, :], (128, 512))
-            hot[pl.ds(at, 128), k * 512 : (k + 1) * 512] = jnp.where(ids == row, 1.0, 0.0).astype(BF16)
+        ids = lax.broadcasted_iota(I32, (128, 128), 0) + at
+        for it in range(4):
+            for k in range(8):
+                row = jnp.broadcast_to(nbr[k : k + 1, it * 128 : (it + 1) * 128], (128, 128))
+                hot[it * 8 + k, pl.ds(at, 128), :] = jnp.where(ids == row, 1.0, 0.0).astype(BF16)
 
 
 def energy_gradient(
-    ext_own, ext_low, ext_up, nb_t, emb, r1, r2, mix1, mix2, rd1, rd2,
+    here, ext_own, ext_low, ext_up, nb_t, emb, r1, r2, mix1, mix2, rd1, rd2,
     to_low, to_up, to_low2, to_up2, kept,
     nb_s, geo, yy, bb, hot, m1, hs, ds1, gg, ww, m2, dg, dw, part, two, dh, dr, fl,
 ):
@@ -143,50 +144,55 @@
         fc = fl[0:1, sl]
         h = e0 + fc * (e1 - e0) + v * sg
         ds1[:, sl] = sg * (1.0 + v * (1.0 - sg))
-        hs[:, sl] = jnp.concatenate(split(h), 0)
+        hh = jnp.concatenate(split(h), 0)
+        for o in range(2):
+            hs[2 * ch + o] = hh[:, o * 128 : (o + 1) * 128]
 
     own_lanes = slice(256, 768)
-    iota8 = lax.broadcasted_iota(I32, (8, 512), 0).astype(F32)
+    iota8 = lax.broadcasted_iota(I32, (8, 256), 0).astype(F32)
     r2th, r2tl = split(colmat[:, 8:16])
     r2lhs = jnp.concatenate([r2th.astype(F32), r2th.astype(F32), r2tl.astype(F32)], 1).astype(BF16)
 
-    def basis(k):
-        off = spread(geo[3, k : k + 1, own_lanes]) - 1.0 - iota8
+    def own_at(it):
+        return slice(256 + it * 128, 384 + it * 128)
+
+    def basis(k, it):
+        row = jnp.concatenate([geo[3, k : k + 1, own_at(it)], geo[3, k + 1 : k + 2, own_at(it)]], 1)
+        off = spread(row) - 1.0 - iota8
         return off, jnp.exp(-0.5 * off * off)
 
-    for k in range(8):
-        gg[k] = halves(dot(hs[...], hot[:, k * 512 : (k + 1) * 512]))
-        _, bk = basis(k)
+    def gather(it, cc):
+        at = it * 8 + 2 * cc
+        feats = jnp.concatenate([hs[t] for t in range(8)], 1)
+        got = halves(dot(feats, jnp.concatenate([hot[at], hot[at + 1]], 1)))
+        _, bk = basis(2 * cc, it)
         bh, bl = split(bk)
         rhs = jnp.concatenate([bh.astype(F32), bl.astype(F32), bh.astype(F32)], 0).astype(BF16)
-        ww[k] = dot(r2lhs, rhs)
+        wgt = dot(r2lhs, rhs)
+        for o in range(2):
+            gg[it, 2 * cc + o] = got[:, o * 128 : (o + 1) * 128]
+            ww[it, 2 * cc + o] = wgt[:, o * 128 : (o + 1) * 128]
 
     def y_row(l, k, it):
-        at = pl.multiple_of(256 + it * 128, 128)
-        return yy[l - 1, k : k + 1, pl.ds(at, 128)]
-
-    @pl.loop(0, 16)
-    def _(step):
-        it = step // 4
-        rows_ = pl.ds(pl.multiple_of((step % 4) * 32, 32), 32)
-        lanes = pl.ds(pl.multiple_of(it * 128, 128), 128)
-        car = [gg[k, rows_, lanes] * ww[k, rows_, lanes] for k in range(8)]
+        return yy[l - 1, k : k + 1, own_at(it)]
+
+    def moments(it, cc):
+        rows_ = slice(cc * 32, cc * 32 + 32)
+        car = [gg[it, k, rows_] * ww[it, k, rows_] for k in range(8)]
         acc = car[0]
         for k in range(1, 8):
             acc = acc + car[k]
-        m2[0, rows_, lanes] = acc
+        m2[it, 0, rows_] = acc
         for l in range(1, 9):
             acc = y_row(l, 0, it) * car[0]
             for k in range(1, 8):
                 acc = acc + y_row(l, k, it) * car[k]
-            m2[l, rows_, lanes] = acc
-
-    @pl.loop(0, 2)
-    def _(ch):
-        sl = pl.ds(pl.multiple_of(ch * 256, 256), 256)
+            m2[it, l, rows_] = acc
+
+    def middle(it):
         q = [None, None, None]
         for l in range(9):
-            m = m2[l, :, sl]
+            m = m2[it, l]
             g = 0 if l == 0 else (1 if l < 4 else 2)
             q[g] = m * m if q[g] is None else q[g] + m * m
         v = mixed(m2s, m2h, jnp.concatenate(q, 0))
@@ -195,20 +201,15 @@
         dq = mixed(m2ts, m2th, dv) * 2.0
         for l in range(9):
             g = 0 if l == 0 else (1 if l < 4 else 2)
-            m2[l, :, sl] = m2[l, :, sl] * dq[g * 128 : (g + 1) * 128]
-
-    part[...] = jnp.zeros_like(part)
-
-    @pl.loop(0, 16)
-    def _(step):
-        it = step // 4
-        at = pl.multiple_of((step % 4) * 32, 32)
-        rows_ = pl.ds(at, 32)
-        rows_lo = pl.ds(at + 128, 32)
-        lanes = pl.ds(pl.multiple_of(it * 128, 128), 128)
-        dm = [m2[l, rows_, lanes] for l in range(9)]
+            m2[it, l] = m2[it, l] * dq[g * 128 : (g + 1) * 128]
+
+    def backward(it, cc):
+        rows_ = slice(cc * 32, cc * 32 + 32)
+        rows_lo = slice(128 + cc * 32, 160 + cc * 32)
+        lanes = slice(it * 128, (it + 1) * 128)
+        dm = [m2[it, l, rows_] for l in range(9)]
         for k in range(8):
-            g, w = gg[k, rows_, lanes], ww[k, rows_, lanes]
+            g, w = gg[it, k, rows_], ww[it, k, rows_]
             car = g * w
             dcar = dm[0]
             for l in range(1, 9):
@@ -217,33 +218,57 @@
                 pr = dm[l] * car
                 pr = (pr[0:8] + pr[8:16]) + (pr[16:24] + pr[24:32])
                 at8 = ((l - 1) * 8 + k) * 8
-                part[at8 : at8 + 8, lanes] = part[at8 : at8 + 8, lanes] + pr
-            edge = pl.ds(pl.multiple_of(k * 512 + it * 128, 128), 128)
+                part[at8 : at8 + 8, lanes] = pr if cc == 0 else part[at8 : at8 + 8, lanes] + pr
             hi, lo = split(dcar * w)
-            dg[rows_, edge] = hi
-            dg[rows_lo, edge] = lo
+            dg[it * 8 + k, rows_] = hi
+            dg[it * 8 + k, rows_lo] = lo
             hi, lo = split(dcar * g)
-            dw[rows_, edge] = hi
-            dw[rows_lo, edge] = lo
-
+            dw[it * 8 + k, rows_] = hi
+            dw[it * 8 + k, rows_lo] = lo
+
+    def scatter(it, cc):
+        cols = slice(cc * 256, (cc + 1) * 256)
+        cot = jnp.concatenate([dg[it * 8 + k] for k in range(8)], 1)
+        res = halves(dot_nt(cot, jnp.concatenate([hot[it * 8 + k, cols] for k in range(8)], 1)))
+        dh[:, cols] = res if it == 0 else dh[:, cols] + res
+
+    for cc in range(4):
+        gather(0, cc)
+    for it in range(4):
+
+        @pl.when(here >= -it)
+        def _():
+            for cc in range(4):
+                if it < 3:
+                    gather(it + 1, cc)
+                moments(it, cc)
+            if it:
+                scatter(it - 1, 0)
+            middle(it)
+            for cc in range(4):
+                if it and cc:
+                    scatter(it - 1, cc)
+                backward(it, cc)
+
+    for cc in range(4):
+        scatter(3, cc)
     r2h, r2l = split(r2s)
     r2f = jnp.concatenate(
         [jnp.concatenate([r2h, r2h], 1).astype(F32), jnp.concatenate([r2l, jnp.zeros_like(r2l)], 1).astype(F32)], 0
     ).astype(BF16)
-    for k in range(8):
-        dbk = halves(dot(r2f, dw[:, k * 512 : (k + 1) * 512]))
-        off, bk = basis(k)
-        part[512 + k * 8 : 520 + k * 8, :] = -(dbk * bk * off)
+    for it in range(4):
+        for cc in range(4):
+            at = it * 8 + 2 * cc
+            dbk = halves(dot(r2f, jnp.concatenate([dw[at], dw[at + 1]], 1)))
+            off, bk = basis(2 * cc, it)
+            res = -(dbk * bk * off)
+            for o in range(2):
+                at = 512 + (2 * cc + o) * 8
+                part[at : at + 8, it * 128 : (it + 1) * 128] = res[:, o * 128 : (o + 1) * 128]
     sel = (lax.broadcasted_iota(I32, (72, 576), 1) >> 3) == lax.broadcasted_iota(I32, (72, 576), 0)
     sel = jnp.where(sel, 1.0, 0.0).astype(BF16)
     ph, pl_ = split(part[...])
-    two[...] = jnp.zeros_like(two)
     two[:, own_lanes] = dot(sel, ph) + dot(sel, pl_)
-
-    @pl.loop(0, 4)
-    def _(ch):
-        at = pl.ds(pl.multiple_of(ch * 256, 256), 256)
-        dh[:, at] = halves(dot_nt(dg[...], hot[at, :]))
 
     @pl.loop(0, 4)
     def _(ch):
@@ -334,15 +359,15 @@
     pltpu.VMEM((6, 8, 1024), F32),
     pltpu.VMEM((8, 8, 1024), F32),
     pltpu.VMEM((8, 8, 1024), F32),
-    pltpu.VMEM((1024, 4096), BF16),
+    pltpu.VMEM((32, 1024, 128), BF16),
     pltpu.VMEM((9, 128, 1024), F32),
-    pltpu.VMEM((256, 1024), BF16),
+    pltpu.VMEM((8, 256, 128), BF16),
     pltpu.VMEM((128, 1024), F32),
-    pltpu.VMEM((8, 128, 512), F32),
-    pltpu.VMEM((8, 128, 512), F32),
-    pltpu.VMEM((9, 128, 512), F32),
-    pltpu.VMEM((256, 4096), BF16),
-    pltpu.VMEM((256, 4096), BF16),
+    pltpu.VMEM((4, 8, 128, 128), F32),
+    pltpu.VMEM((4, 8, 128, 128), F32),
+    pltpu.VMEM((4, 9, 128, 128), F32),
+    pltpu.VMEM((32, 256, 128), BF16),
+    pltpu.VMEM((32, 256, 128), BF16),
     pltpu.VMEM((576, 512), F32),
     pltpu.VMEM((72, 1024), F32),
     pltpu.VMEM((128, 1024), F32),
@@ -442,6 +467,8 @@
         (msg_up, msg_low, msg_up.at[16:24], msg_low.at[16:24]), (in_low, in_up, in_low2, in_up2), fs_sem, fr_sem
     )
     build_hot(nbr, work[4])
+    two = work[14]
+    two[...] = jnp.zeros_like(two)
     for c in halo:
         c.wait()
     q_copies = share(q_src, q_all, qs_sem, qr_sem)
@@ -455,7 +482,7 @@
     nb_t = [in_low[24:32, :].astype(I32), in_low[32:40, :].astype(I32)] + nbr_t
     nb_t = nb_t + [in_up[24:32, :].astype(I32), in_up[32:40, :].astype(I32)]
     energy_gradient(
-        ext_own, ext_low, ext_up, nb_t, emb, r1, r2, mix1, mix2, rd1, rd2,
+        me, ext_own, ext_low, ext_up, nb_t, emb, r1, r2, mix1, mix2, rd1, rd2,
         to_low, to_up, to_low2, to_up2, kept, *work,
     )
     copies = to_near(

time: 59.1 us -> 56.6 us (0.958)
  Pallas kernels: 56.3 us -> 53.8 us
    pallas_call x1, Pallas kernels: 56.3 us -> 53.8 us  [shards(): pl.pallas_call(lambda *refs: step_kernel(domains, beads, *refs), out_shap...]
where the time goes in v3:
time: 56.6 us; the launch traced here: 56.4 us
  Pallas kernels  53.8 us (95%)
  local copies, waits for them, and re-layouts  1.97 us (3%)
  between operations  0.65 us (1%)
    pallas_call x1, Pallas kernels, shards(): pl.pallas_call(lambda *refs: step_kernel(domains, beads, *refs), out_shap...  53.8 us
    unnamed x6, local copies, waits for them, and re-layouts  1.97 us

profile of v3, /device:TPU:1, one launch (start us, length us, event | category | flops | bytes accessed | tf_op | source)
XLA Modules:
  0.0 56.4 jit_solution(7117463419556403518)
XLA Ops:
  0.6 53.8 %md_step.1 = (f32[3,1,512]{2,1,0:T(1,128)}, f32[3,1,512]{2,1,0:T(1,128)}) custom-call(f32[3,1,512]{2,1,0:T(1,128)} %bitcast.10, f32[3,1,512]{2,1,0:T(1,128)} %bitcast.11, s32[1,512]{1,0:T(1,128)} %bitcast.12, s32[8,512]{1,0:T(8,128)} %refs_3_.1, s32[1,512]{1,0:T(1,128)} %bitcast.13, f32[2,128]{1,0:T(2,128)} %refs_5_.1, f32[8,128]{1,0:T(8,128)} %refs_6_.1, ...), custom_call_target="tpu_custom_call" | custom-call | tf_op jit(solution)/shard_map/md_step/pallas_call | solution.py:551
  54.5 0.0 copy-start.1
  54.5 0.7 %copy-done.1 = f32[3,1,512]{2,1,0:T(1,128)S(1)} copy-done((f32[3,1,512]{2,1,0:T(1,128)S(1)}, f32[3,1,512]{2,1,0:T(1,128)}, u32[]{:S(2)}) %copy-start.1) | copy-done | bytes 6168
  55.2 0.0 copy-start
  55.2 0.6 %copy.16 = f32[1,3,512]{2,0,1:T(1,128)} copy(f32[1,3,512]{2,0,1:T(1,128)S(1)} %bitcast.9) | data formatting | bytes 12288
  55.7 0.1 copy-done
  55.9 0.6 %copy.17 = f32[1,3,512]{2,0,1:T(1,128)} copy(f32[1,3,512]{2,0,1:T(1,128)S(1)} %bitcast.8) | data formatting | bytes 12288
Async XLA Ops:
  54.5 0.7 %copy-start.1 = (f32[3,1,512]{2,1,0:T(1,128)S(1)}, f32[3,1,512]{2,1,0:T(1,128)}, u32[]{:S(2)}) copy-start(f32[3,1,512]{2,1,0:T(1,128)} %get-tuple-element.4) | copy-start | bytes 18436
  55.2 0.7 %copy-start = (f32[3,1,512]{2,1,0:T(1,128)S(1)}, f32[3,1,512]{2,1,0:T(1,128)}, u32[]{:S(2)}) copy-start(f32[3,1,512]{2,1,0:T(1,128)} %get-tuple-element.5) | copy-start | bytes 18436

commit v4 on v3

--- a/solution.py
+++ b/solution.py
@@ -65,35 +65,17 @@
                 hot[it * 8 + k, pl.ds(at, 128), :] = jnp.where(ids == row, 1.0, 0.0).astype(BF16)
 
 
-def energy_gradient(
-    here, ext_own, ext_low, ext_up, nb_t, emb, r1, r2, mix1, mix2, rd1, rd2,
-    to_low, to_up, to_low2, to_up2, kept,
-    nb_s, geo, yy, bb, hot, m1, hs, ds1, gg, ww, m2, dg, dw, part, two, dh, dr, fl,
-):
-    for e in range(8):
-        cols = slice(e * 128, (e + 1) * 128)
-        ext = ext_low if e < 2 else (ext_own if e < 6 else ext_up)
-        idx = nb_t[e]
-        nb_s[:, cols] = idx
-        fl[:, cols] = spread(ext_own[e][3:4])
-        got = [lane_take([spread(x[c : c + 1]) for x in ext], idx) for c in range(4)]
-        rx, ry, rz = [got[c] - spread(ext_own[e][c : c + 1]) for c in range(3)]
-        s = jnp.sqrt(rx * rx + ry * ry + rz * rz + 1.0)
-        inv = 1.0 / s
-        ux, uy, uz = rx * inv, ry * inv, rz * inv
-        for c, v in enumerate((ux, uy, uz, s, inv, got[3])):
-            geo[c, :, cols] = v
-        ys = (
-            SQRT3 * ux, SQRT3 * uy, SQRT3 * uz,
-            SQRT15 * ux * uy, SQRT15 * uy * uz,
-            0.5 * SQRT5 * (2.0 * uz * uz - ux * ux - uy * uy),
-            SQRT15 * ux * uz, 0.5 * SQRT15 * (ux * ux - uy * uy),
-        )
-        for l in range(8):
-            yy[l, :, cols] = ys[l]
-        for n in range(8):
-            bb[n, :, cols] = jnp.exp(-0.5 * (s - (1.0 + n)) ** 2)
-
+def prepare(nbr, weights, work):
+    emb, r1, r2, mix1, mix2, rd1, rd2 = weights
+    hot, two, lam = work[4], work[14], work[18]
+    build_hot(nbr, hot)
+    two[...] = jnp.zeros_like(two)
+    lane_ids = lax.broadcasted_iota(I32, (128, 512), 0)
+    for k in range(8):
+        row = jnp.broadcast_to(nbr[k : k + 1, :] & 127, (128, 512))
+        one = jnp.where(row == lane_ids, 1.0, 0.0).astype(BF16)
+        for t in range(4):
+            lam[k * 4 + t] = one[:, t * 128 : (t + 1) * 128]
     w_rows = []
     for f in range(2):
         for n in range(8):
@@ -118,12 +100,50 @@
     m2s = jnp.concatenate([m2h, m2l], 0)
     m2th, m2tl = split(jnp.transpose(mix2[...]))
     m2ts = jnp.concatenate([m2th, m2tl], 0)
+    r2th, r2tl = split(colmat[:, 8:16])
+    r2lhs = jnp.concatenate([r2th.astype(F32), r2th.astype(F32), r2tl.astype(F32)], 1).astype(BF16)
+    r2h, r2l = split(r2s)
+    r2f = jnp.concatenate(
+        [jnp.concatenate([r2h, r2h], 1).astype(F32), jnp.concatenate([r2l, jnp.zeros_like(r2l)], 1).astype(F32)], 0
+    ).astype(BF16)
+    return wf, wtf, e0, e1, c_rd1, c_rd2, m1h, m1s, m1th, m1ts, m2h, m2s, m2th, m2ts, r2s, r2lhs, r2f
+
+
+def energy_gradient(
+    prepared, ext_own, ext_low, ext_up, nb_t,
+    to_low, to_up, to_low2, to_up2, kept,
+    nb_s, geo, yy, bb, hot, m1, hs, ds1, gg, ww, m2, dg, dw, part, two, dh, dr, fl, lam,
+):
+    (wf, wtf, e0, e1, c_rd1, c_rd2, m1h, m1s, m1th, m1ts, m2h, m2s, m2th, m2ts, r2s, r2lhs, r2f) = prepared
+    for e in range(8):
+        cols = slice(e * 128, (e + 1) * 128)
+        ext = ext_low if e < 2 else (ext_own if e < 6 else ext_up)
+        idx = nb_t[e]
+        nb_s[:, cols] = idx
+        fl[:, cols] = spread(ext_own[e][3:4])
+        got = [lane_take([spread(x[c : c + 1]) for x in ext], idx) for c in range(4)]
+        rx, ry, rz = [got[c] - spread(ext_own[e][c : c + 1]) for c in range(3)]
+        s = jnp.sqrt(rx * rx + ry * ry + rz * rz + 1.0)
+        inv = 1.0 / s
+        ux, uy, uz = rx * inv, ry * inv, rz * inv
+        for c, v in enumerate((ux, uy, uz, s, inv, got[3])):
+            geo[c, :, cols] = v
+        ys = (
+            SQRT3 * ux, SQRT3 * uy, SQRT3 * uz,
+            SQRT15 * ux * uy, SQRT15 * uy * uz,
+            0.5 * SQRT5 * (2.0 * uz * uz - ux * ux - uy * uy),
+            SQRT15 * ux * uz, 0.5 * SQRT15 * (ux * ux - uy * uy),
+        )
+        for l in range(8):
+            yy[l, :, cols] = ys[l]
+        for n in range(8):
+            bb[n, :, cols] = jnp.exp(-0.5 * (s - (1.0 + n)) ** 2)
 
     def mixed(ws, wh_, x):
         hi, lo = split(x)
         return halves(dot(ws, hi)) + dot(wh_, lo)
 
-    @pl.loop(0, 4)
+    @pl.loop(0, 4, unroll=2)
     def _(ch):
         sl = pl.ds(pl.multiple_of(ch * 256, 256), 256)
         f = geo[5, :, sl]
@@ -150,8 +170,6 @@
 
     own_lanes = slice(256, 768)
     iota8 = lax.broadcasted_iota(I32, (8, 256), 0).astype(F32)
-    r2th, r2tl = split(colmat[:, 8:16])
-    r2lhs = jnp.concatenate([r2th.astype(F32), r2th.astype(F32), r2tl.astype(F32)], 1).astype(BF16)
 
     def own_at(it):
         return slice(256 + it * 128, 384 + it * 128)
@@ -235,27 +253,19 @@
     for cc in range(4):
         gather(0, cc)
     for it in range(4):
-
-        @pl.when(here >= -it)
-        def _():
-            for cc in range(4):
-                if it < 3:
-                    gather(it + 1, cc)
-                moments(it, cc)
+        for cc in range(4):
+            if it < 3:
+                gather(it + 1, cc)
+            moments(it, cc)
+    for it in range(4):
+        middle(it)
+    for it in range(4):
+        for cc in range(4):
             if it:
-                scatter(it - 1, 0)
-            middle(it)
-            for cc in range(4):
-                if it and cc:
-                    scatter(it - 1, cc)
-                backward(it, cc)
-
+                scatter(it - 1, cc)
+            backward(it, cc)
     for cc in range(4):
         scatter(3, cc)
-    r2h, r2l = split(r2s)
-    r2f = jnp.concatenate(
-        [jnp.concatenate([r2h, r2h], 1).astype(F32), jnp.concatenate([r2l, jnp.zeros_like(r2l)], 1).astype(F32)], 0
-    ).astype(BF16)
     for it in range(4):
         for cc in range(4):
             at = it * 8 + 2 * cc
@@ -270,7 +280,7 @@
     ph, pl_ = split(part[...])
     two[:, own_lanes] = dot(sel, ph) + dot(sel, pl_)
 
-    @pl.loop(0, 4)
+    @pl.loop(0, 4, unroll=2)
     def _(ch):
         sl = pl.ds(pl.multiple_of(ch * 256, 256), 256)
         is_own = jnp.where(jnp.logical_or(ch == 1, ch == 2), 1.0, 0.0).astype(F32)
@@ -308,31 +318,32 @@
         dr[2, :, sl] = duz * inv + uz * along
 
     tile_ids = lax.broadcasted_iota(I32, (8, 1024), 0)
-    lane_ids = lax.broadcasted_iota(I32, (128, 1024), 0)
-
-    def onto(index_row, values):
-        there = spread(index_row >> 7) == tile_ids
+    lane_ids = lax.broadcasted_iota(I32, (128, 256), 0)
+    acc_own = jnp.zeros((48, 128), F32)
+    acc_low = jnp.zeros((48, 128), F32)
+    acc_up = jnp.zeros((48, 128), F32)
+    for k in range(8):
+        row = nb_s[k : k + 1, :]
+        there = spread(row >> 7) == tile_ids
         his, los = [], []
-        for v in values:
-            m = jnp.where(there, spread(v), 0.0)
+        for c in range(3):
+            m = jnp.where(there, spread(dr[c, k : k + 1, :]), 0.0)
             hi = m.astype(BF16).astype(F32)
             his.append(hi)
             los.append(m - hi)
         lhs = jnp.concatenate(his + los, 0).astype(BF16)
-        rhs = jnp.where(jnp.broadcast_to(index_row & 127, (128, 1024)) == lane_ids, 1.0, 0.0).astype(BF16)
-        return lhs, rhs
-
-    selfs = lax.broadcasted_iota(I32, (1, 1024), 1)
-    lhs, rhs = onto(selfs, [-jnp.sum(dr[c], axis=0, keepdims=True) for c in range(3)])
-    acc_own = dot_nt(lhs, rhs)
-    acc_low = jnp.zeros((48, 128), F32)
-    acc_up = jnp.zeros((48, 128), F32)
-    for k in range(8):
-        lhs, rhs = onto(nb_s[k : k + 1, :], [dr[c, k : k + 1, :] for c in range(3)])
-        acc_own = acc_own + dot_nt(lhs[:, 256:768], rhs[:, 256:768])
-        acc_low = acc_low + dot_nt(lhs[:, :256], rhs[:, :256])
-        acc_up = acc_up + dot_nt(lhs[:, 768:], rhs[:, 768:])
-    acc_own, acc_low, acc_up = halves(acc_own), halves(acc_low), halves(acc_up)
+
+        def ghost(first):
+            part_ = jnp.broadcast_to(row[:, first : first + 256] & 127, (128, 256))
+            return jnp.where(part_ == lane_ids, 1.0, 0.0).astype(BF16)
+
+        own_hot = jnp.concatenate([lam[k * 4 + t] for t in range(4)], 1)
+        acc_own = acc_own + dot_nt(lhs[:, 256:768], own_hot)
+        acc_low = acc_low + dot_nt(lhs[:, :256], ghost(0))
+        acc_up = acc_up + dot_nt(lhs[:, 768:], ghost(768))
+    selfs = [jnp.sum(dr[c], axis=0, keepdims=True) for c in range(3)]
+    selfs = jnp.concatenate([v[:, t * 128 : (t + 1) * 128] for v in selfs for t in range(8)], 0)
+    acc_own, acc_low, acc_up = halves(acc_own) - selfs, halves(acc_low), halves(acc_up)
 
     def put(ref, at, acc, c, first, count):
         ref[at : at + count, :] = acc[c * 8 + first : c * 8 + first + count, :]
@@ -373,6 +384,7 @@
     pltpu.VMEM((128, 1024), F32),
     pltpu.VMEM((3, 8, 1024), F32),
     pltpu.VMEM((8, 1024), F32),
+    pltpu.VMEM((32, 128, 128), BF16),
 ]
 
 
@@ -466,12 +478,10 @@
     halo = to_near(
         (msg_up, msg_low, msg_up.at[16:24], msg_low.at[16:24]), (in_low, in_up, in_low2, in_up2), fs_sem, fr_sem
     )
-    build_hot(nbr, work[4])
-    two = work[14]
-    two[...] = jnp.zeros_like(two)
+    prepared = prepare(nbr, (emb, r1, r2, mix1, mix2, rd1, rd2), work)
+    q_copies = share(q_src, q_all, qs_sem, qr_sem)
     for c in halo:
         c.wait()
-    q_copies = share(q_src, q_all, qs_sem, qr_sem)
 
     def whole(ref):
         return both(ref[0:8, :]) + both(ref[8:16, :])
@@ -482,8 +492,7 @@
     nb_t = [in_low[24:32, :].astype(I32), in_low[32:40, :].astype(I32)] + nbr_t
     nb_t = nb_t + [in_up[24:32, :].astype(I32), in_up[32:40, :].astype(I32)]
     energy_gradient(
-        me, ext_own, ext_low, ext_up, nb_t, emb, r1, r2, mix1, mix2, rd1, rd2,
-        to_low, to_up, to_low2, to_up2, kept, *work,
+        prepared, ext_own, ext_low, ext_up, nb_t, to_low, to_up, to_low2, to_up2, kept, *work,
     )
     copies = to_near(
         (to_up, to_low, to_up2, to_low2), (from_low, from_up, from_low2, from_up2), hs_sem, hr_sem

time: 56.6 us -> 50.9 us (0.90)
  Pallas kernels: 53.8 us -> 48.1 us
    pallas_call x1, Pallas kernels: 53.8 us -> 48.1 us  [shards(): pl.pallas_call(lambda *refs: step_kernel(domains, beads, *refs), out_shap...]
where the time goes in v4:
time: 50.9 us; the launch traced here: 50.7 us
  Pallas kernels  48.1 us (94%)
  local copies, waits for them, and re-layouts  1.97 us (4%)
  between operations  0.65 us (1%)
    pallas_call x1, Pallas kernels, shards(): pl.pallas_call(lambda *refs: step_kernel(domains, beads, *refs), out_shap...  48.1 us
    unnamed x6, local copies, waits for them, and re-layouts  1.97 us

profile of v4, /device:TPU:1, one launch (start us, length us, event | category | flops | bytes accessed | tf_op | source)
XLA Modules:
  0.0 50.7 jit_solution(7125083456727918754)
XLA Ops:
  0.6 48.1 %md_step.1 = (f32[3,1,512]{2,1,0:T(1,128)}, f32[3,1,512]{2,1,0:T(1,128)}) custom-call(f32[3,1,512]{2,1,0:T(1,128)} %bitcast.10, f32[3,1,512]{2,1,0:T(1,128)} %bitcast.11, s32[1,512]{1,0:T(1,128)} %bitcast.12, s32[8,512]{1,0:T(8,128)} %refs_3_.1, s32[1,512]{1,0:T(1,128)} %bitcast.13, f32[2,128]{1,0:T(2,128)} %refs_5_.1, f32[8,128]{1,0:T(8,128)} %refs_6_.1, ...), custom_call_target="tpu_custom_call" | custom-call | tf_op jit(solution)/shard_map/md_step/pallas_call | solution.py:560
  48.7 0.0 copy-start.1
  48.8 0.7 %copy-done.1 = f32[3,1,512]{2,1,0:T(1,128)S(1)} copy-done((f32[3,1,512]{2,1,0:T(1,128)S(1)}, f32[3,1,512]{2,1,0:T(1,128)}, u32[]{:S(2)}) %copy-start.1) | copy-done | bytes 6168
  49.4 0.0 copy-start
  49.4 0.6 %copy.16 = f32[1,3,512]{2,0,1:T(1,128)} copy(f32[1,3,512]{2,0,1:T(1,128)S(1)} %bitcast.9) | data formatting | bytes 12288
  50.0 0.1 copy-done
  50.1 0.6 %copy.17 = f32[1,3,512]{2,0,1:T(1,128)} copy(f32[1,3,512]{2,0,1:T(1,128)S(1)} %bitcast.8) | data formatting | bytes 12288
Async XLA Ops:
  48.7 0.7 %copy-start.1 = (f32[3,1,512]{2,1,0:T(1,128)S(1)}, f32[3,1,512]{2,1,0:T(1,128)}, u32[]{:S(2)}) copy-start(f32[3,1,512]{2,1,0:T(1,128)} %get-tuple-element.4) | copy-start | bytes 18436
  49.4 0.7 %copy-start = (f32[3,1,512]{2,1,0:T(1,128)S(1)}, f32[3,1,512]{2,1,0:T(1,128)}, u32[]{:S(2)}) copy-start(f32[3,1,512]{2,1,0:T(1,128)} %get-tuple-element.5) | copy-start | bytes 18436

commit v5 on v4

--- a/solution.py
+++ b/solution.py
@@ -110,15 +110,13 @@
 
 
 def energy_gradient(
-    prepared, ext_own, ext_low, ext_up, nb_t,
-    to_low, to_up, to_low2, to_up2, kept,
-    nb_s, geo, yy, bb, hot, m1, hs, ds1, gg, ww, m2, dg, dw, part, two, dh, dr, fl, lam,
+    here, prepared, ext_own, nb_own, rest, send_early,
+    to_low, to_up, to_low2, to_up2, to_low_s, to_up_s, kept,
+    nb_s, geo, yy, bb, hot, m1, hs, ds1, gg, ww, m2, dg, dw, part, two, dh, dr, fl, lam, lam_g,
 ):
     (wf, wtf, e0, e1, c_rd1, c_rd2, m1h, m1s, m1th, m1ts, m2h, m2s, m2th, m2ts, r2s, r2lhs, r2f) = prepared
-    for e in range(8):
+    def geometry(e, ext, idx):
         cols = slice(e * 128, (e + 1) * 128)
-        ext = ext_low if e < 2 else (ext_own if e < 6 else ext_up)
-        idx = nb_t[e]
         nb_s[:, cols] = idx
         fl[:, cols] = spread(ext_own[e][3:4])
         got = [lane_take([spread(x[c : c + 1]) for x in ext], idx) for c in range(4)]
@@ -143,9 +141,8 @@
         hi, lo = split(x)
         return halves(dot(ws, hi)) + dot(wh_, lo)
 
-    @pl.loop(0, 4, unroll=2)
-    def _(ch):
-        sl = pl.ds(pl.multiple_of(ch * 256, 256), 256)
+    def forward(ch):
+        sl = slice(ch * 256, (ch + 1) * 256)
         f = geo[5, :, sl]
         bs = []
         for n in range(8):
@@ -167,6 +164,29 @@
         hh = jnp.concatenate(split(h), 0)
         for o in range(2):
             hs[2 * ch + o] = hh[:, o * 128 : (o + 1) * 128]
+
+    for e in range(2, 6):
+        geometry(e, ext_own, nb_own[e - 2])
+
+    @pl.when(here >= 0)
+    def _():
+        forward(1)
+        forward(2)
+
+    ext_low, ext_up, nb_ghost = rest()
+    for o, e in enumerate((0, 1, 6, 7)):
+        geometry(e, ext_low if e < 2 else ext_up, nb_ghost[o])
+
+    @pl.when(here >= -1)
+    def _():
+        forward(0)
+        forward(3)
+
+    lane_ids = lax.broadcasted_iota(I32, (128, 128), 0)
+    for k in range(8):
+        for o, e in enumerate((0, 1, 6, 7)):
+            row = jnp.broadcast_to(nb_s[k : k + 1, e * 128 : (e + 1) * 128] & 127, (128, 128))
+            lam_g[k * 4 + o] = jnp.where(row == lane_ids, 1.0, 0.0).astype(BF16)
 
     own_lanes = slice(256, 768)
     iota8 = lax.broadcasted_iota(I32, (8, 256), 0).astype(F32)
@@ -280,11 +300,9 @@
     ph, pl_ = split(part[...])
     two[:, own_lanes] = dot(sel, ph) + dot(sel, pl_)
 
-    @pl.loop(0, 4, unroll=2)
-    def _(ch):
-        sl = pl.ds(pl.multiple_of(ch * 256, 256), 256)
-        is_own = jnp.where(jnp.logical_or(ch == 1, ch == 2), 1.0, 0.0).astype(F32)
-        dv = (dh[:, sl] + c_rd1 * is_own) * ds1[:, sl]
+    def backward_one(ch):
+        sl = slice(ch * 256, (ch + 1) * 256)
+        dv = (dh[:, sl] + c_rd1 if ch in (1, 2) else dh[:, sl]) * ds1[:, sl]
         dq = mixed(m1ts, m1th, dv) * 2.0
         on = geo[5, :, sl] > 0.5
         ux, uy, uz = geo[0, :, sl], geo[1, :, sl], geo[2, :, sl]
@@ -317,52 +335,57 @@
         dr[1, :, sl] = duy * inv + uy * along
         dr[2, :, sl] = duz * inv + uz * along
 
-    tile_ids = lax.broadcasted_iota(I32, (8, 1024), 0)
-    lane_ids = lax.broadcasted_iota(I32, (128, 256), 0)
-    acc_own = jnp.zeros((48, 128), F32)
-    acc_low = jnp.zeros((48, 128), F32)
-    acc_up = jnp.zeros((48, 128), F32)
-    for k in range(8):
-        row = nb_s[k : k + 1, :]
-        there = spread(row >> 7) == tile_ids
-        his, los = [], []
-        for c in range(3):
-            m = jnp.where(there, spread(dr[c, k : k + 1, :]), 0.0)
-            hi = m.astype(BF16).astype(F32)
-            his.append(hi)
-            los.append(m - hi)
-        lhs = jnp.concatenate(his + los, 0).astype(BF16)
-
-        def ghost(first):
-            part_ = jnp.broadcast_to(row[:, first : first + 256] & 127, (128, 256))
-            return jnp.where(part_ == lane_ids, 1.0, 0.0).astype(BF16)
-
-        own_hot = jnp.concatenate([lam[k * 4 + t] for t in range(4)], 1)
-        acc_own = acc_own + dot_nt(lhs[:, 256:768], own_hot)
-        acc_low = acc_low + dot_nt(lhs[:, :256], ghost(0))
-        acc_up = acc_up + dot_nt(lhs[:, 768:], ghost(768))
-    selfs = [jnp.sum(dr[c], axis=0, keepdims=True) for c in range(3)]
-    selfs = jnp.concatenate([v[:, t * 128 : (t + 1) * 128] for v in selfs for t in range(8)], 0)
-    acc_own, acc_low, acc_up = halves(acc_own) - selfs, halves(acc_low), halves(acc_up)
+    def onto(first, count, hots):
+        tile_ids = lax.broadcasted_iota(I32, (8, count), 0)
+        acc = jnp.zeros((48, 128), F32)
+        for k in range(8):
+            there = spread(nb_s[k : k + 1, first : first + count] >> 7) == tile_ids
+            his, los = [], []
+            for c in range(3):
+                m = jnp.where(there, spread(dr[c, k : k + 1, first : first + count]), 0.0)
+                hi = m.astype(BF16).astype(F32)
+                his.append(hi)
+                los.append(m - hi)
+            lhs = jnp.concatenate(his + los, 0).astype(BF16)
+            acc = acc + dot_nt(lhs, jnp.concatenate(hots(k), 1))
+        return halves(acc)
 
     def put(ref, at, acc, c, first, count):
         ref[at : at + count, :] = acc[c * 8 + first : c * 8 + first + count, :]
 
+    for ref in (to_low2, to_up2, to_low_s, to_up_s):
+        ref[6:8, :] = jnp.zeros((2, 128), F32)
+    for ref in (to_low, to_up):
+        ref[12:16, :] = jnp.zeros((4, 128), F32)
+
+    @pl.when(here >= 0)
+    def _():
+        backward_one(0)
+        backward_one(3)
+
+    acc_low = onto(0, 256, lambda k: [lam_g[k * 4], lam_g[k * 4 + 1]])
+    acc_up = onto(768, 256, lambda k: [lam_g[k * 4 + 2], lam_g[k * 4 + 3]])
     for c in range(3):
-        put(kept, c * 4, acc_own, c, 2, 4)
         put(kept, 12 + c * 4, acc_low, c, 6, 2)
         put(kept, 14 + c * 4, acc_up, c, 0, 2)
         put(to_low, c * 4, acc_low, c, 2, 4)
-        put(to_low, 12 + c * 2, acc_own, c, 0, 2)
         put(to_up, c * 4, acc_up, c, 2, 4)
-        put(to_up, 12 + c * 2, acc_own, c, 6, 2)
         put(to_low2, c * 2, acc_low, c, 0, 2)
         put(to_up2, c * 2, acc_up, c, 6, 2)
-    pad2, pad6 = jnp.zeros((2, 128), F32), jnp.zeros((6, 128), F32)
-    to_low[18:24, :] = pad6
-    to_up[18:24, :] = pad6
-    to_low2[6:8, :] = pad2
-    to_up2[6:8, :] = pad2
+    send_early()
+
+    @pl.when(here >= -1)
+    def _():
+        backward_one(1)
+        backward_one(2)
+
+    selfs = [jnp.sum(dr[c], axis=0, keepdims=True) for c in range(3)]
+    selfs = jnp.concatenate([v[:, t * 128 : (t + 1) * 128] for v in selfs for t in range(8)], 0)
+    acc_own = onto(256, 512, lambda k: [lam[k * 4 + t] for t in range(4)]) - selfs
+    for c in range(3):
+        put(kept, c * 4, acc_own, c, 2, 4)
+        put(to_low_s, c * 2, acc_own, c, 0, 2)
+        put(to_up_s, c * 2, acc_own, c, 6, 2)
 
 
 COMPUTE_SCRATCH = [
@@ -385,6 +408,7 @@
     pltpu.VMEM((3, 8, 1024), F32),
     pltpu.VMEM((8, 1024), F32),
     pltpu.VMEM((32, 128, 128), BF16),
+    pltpu.VMEM((32, 128, 128), BF16),
 ]
 
 
@@ -405,10 +429,10 @@
 def step_kernel(
     domains, beads,
     pos, mom, spec, nbr, send_ref, emb, r1, r2, mix1, mix2, rd1, rd2,
-    new_pos, new_mom,
+    packed,
     msg_up, msg_low, in_low, in_up, in_low2, in_up2,
-    to_low, to_up, to_low2, to_up2, kept,
-    from_low, from_up, from_low2, from_up2, q_src, p_src, q_all, p_all,
+    to_low, to_up, to_low2, to_up2, to_low_s, to_up_s, kept,
+    from_low, from_up, from_low2, from_up2, from_low_s, from_up_s, q_src, p_src, q_all, p_all,
     fs_sem, fr_sem, hs_sem, hr_sem, qs_sem, qr_sem, ps_sem, pr_sem,
     *work,
 ):
@@ -446,16 +470,16 @@
     q_src[...] = rows12(pos)
     for msg, half in ((msg_low, 0), (msg_up, 1)):
         lists = sent(nbr_t, half)
-        msg[0:8, :] = pair(own_t[0], own_t[1])
-        msg[8:16, :] = pair(own_t[2], own_t[3])
-        msg[16:24, :] = pair(*ghosts[half])
+        msg[0:8, :] = pair(*ghosts[half])
+        msg[8:16, :] = pair(own_t[0], own_t[1])
+        msg[16:24, :] = pair(own_t[2], own_t[3])
         msg[24:32, :] = lists[0].astype(F32)
         msg[32:40, :] = lists[1].astype(F32)
     pl.semaphore_wait(barrier, 4 + beads - 1)
 
-    def to_near(srcs, dsts, s_sem, r_sem):
+    def to_near(first, peers, srcs, dsts, s_sem, r_sem):
         out = []
-        for i, (p, s, dst) in enumerate(zip(near, srcs, dsts)):
+        for i, p, s, dst in zip(range(first, 6), peers, srcs, dsts):
             c = pltpu.make_async_remote_copy(
                 src_ref=s, dst_ref=dst, send_sem=s_sem.at[i], recv_sem=r_sem.at[i],
                 device_id={"space": p}, device_id_type=MESH,
@@ -475,8 +499,11 @@
             out.append(c)
         return out
 
-    halo = to_near(
-        (msg_up, msg_low, msg_up.at[16:24], msg_low.at[16:24]), (in_low, in_up, in_low2, in_up2), fs_sem, fr_sem
+    edge = (msg_up.at[0:8], msg_low.at[0:8])
+    halo = to_near(0, near, edge, (in_low.at[0:8], in_up.at[0:8]), fs_sem, fr_sem)
+    bulk = to_near(
+        2, near, (msg_up.at[8:40], msg_low.at[8:40]) + edge, (in_low.at[8:40], in_up.at[8:40], in_low2, in_up2),
+        fs_sem, fr_sem,
     )
     prepared = prepare(nbr, (emb, r1, r2, mix1, mix2, rd1, rd2), work)
     q_copies = share(q_src, q_all, qs_sem, qr_sem)
@@ -484,19 +511,28 @@
         c.wait()
 
     def whole(ref):
-        return both(ref[0:8, :]) + both(ref[8:16, :])
-
-    ext_own = both(in_low[16:24, :]) + own_t + both(in_up[16:24, :])
-    ext_low = both(in_low2[...]) + whole(in_low) + ghosts[0]
-    ext_up = ghosts[1] + whole(in_up) + both(in_up2[...])
-    nb_t = [in_low[24:32, :].astype(I32), in_low[32:40, :].astype(I32)] + nbr_t
-    nb_t = nb_t + [in_up[24:32, :].astype(I32), in_up[32:40, :].astype(I32)]
+        return both(ref[8:16, :]) + both(ref[16:24, :])
+
+    def rest():
+        for c in bulk:
+            c.wait()
+        ext_low = both(in_low2[...]) + whole(in_low) + ghosts[0]
+        ext_up = ghosts[1] + whole(in_up) + both(in_up2[...])
+        return ext_low, ext_up, [r[a : a + 8, :].astype(I32) for r in (in_low, in_up) for a in (24, 32)]
+
+    copies = []
+
+    def send_early():
+        copies.extend(
+            to_near(0, near, (to_up, to_low, to_up2, to_low2), (from_low, from_up, from_low2, from_up2), hs_sem, hr_sem)
+        )
+
+    ext_own = both(in_low[0:8, :]) + own_t + both(in_up[0:8, :])
     energy_gradient(
-        prepared, ext_own, ext_low, ext_up, nb_t, to_low, to_up, to_low2, to_up2, kept, *work,
+        me, prepared, ext_own, nbr_t, rest, send_early,
+        to_low, to_up, to_low2, to_up2, to_low_s, to_up_s, kept, *work,
     )
-    copies = to_near(
-        (to_up, to_low, to_up2, to_low2), (from_low, from_up, from_low2, from_up2), hs_sem, hr_sem
-    )
+    copies += to_near(4, near, (to_up_s, to_low_s), (from_low_s, from_up_s), hs_sem, hr_sem)
 
     there = [spread(send[:, t * 128 : (t + 1) * 128] >> 7) for t in range(4)]
     iota8 = lax.broadcasted_iota(I32, (8, 128), 0)
@@ -515,9 +551,9 @@
     for c in range(3):
         parts = []
         for t in range(4):
-            near_, far = (from_low, from_low2) if t < 2 else (from_up, from_up2)
-            at, a12, a2 = 12 + c * 4 + t, 12 + c * 2 + t % 2, c * 2 + t % 2
-            v = kept[at : at + 1, :] + near_[a12 : a12 + 1, :] + far[a2 : a2 + 1, :]
+            near_, far = (from_low_s, from_low2) if t < 2 else (from_up_s, from_up2)
+            at, a2 = 12 + c * 4 + t, c * 2 + t % 2
+            v = kept[at : at + 1, :] + near_[a2 : a2 + 1, :] + far[a2 : a2 + 1, :]
             parts.append(jnp.where(there[t] == iota8, spread(v), 0.0))
         m = jnp.concatenate(parts, 1)
         hi = m.astype(BF16).astype(F32)
@@ -541,13 +577,11 @@
         c.wait()
         p = p_all[o]
         pa, pr = pa + turn[o] * p, pr + reach[o] * p
-    qn = qa + pr / mass
-    pn = pa - mass * qs
-    for c in range(3):
-        for t in range(4):
-            at = c * 4 + t
-            new_pos[c, 0:1, t * 128 : (t + 1) * 128] = qn[at : at + 1]
-            new_mom[c, 0:1, t * 128 : (t + 1) * 128] = pn[at : at + 1]
+    for i, v in enumerate((qa, pr / mass, pa, mass * qs)):
+        for c in range(3):
+            for t in range(4):
+                at = c * 4 + t
+                packed[i, c, 0:1, t * 128 : (t + 1) * 128] = v[at : at + 1]
 
 
 def shards(
@@ -557,14 +591,14 @@
     domains, beads = lax.axis_size("space"), lax.axis_size("bead")
     dma = lambda n: pltpu.SemaphoreType.DMA((n,))
     rows = lambda n: pltpu.VMEM((n, 128), F32)
-    q, p = pl.pallas_call(
+    out = pl.pallas_call(
         lambda *refs: step_kernel(domains, beads, *refs),
-        out_shape=(jax.ShapeDtypeStruct((3, 1, 512), F32),) * 2,
+        out_shape=jax.ShapeDtypeStruct((4, 3, 1, 512), F32),
         in_specs=[VM] * 12,
-        out_specs=(VM,) * 2,
-        scratch_shapes=[rows(n) for n in (40, 40, 40, 40, 8, 8, 24, 24, 8, 8, 24, 24, 24, 8, 8, 12, 12)]
+        out_specs=VM,
+        scratch_shapes=[rows(n) for n in (40, 40, 40, 40, 8, 8, 16, 16, 8, 8, 8, 8, 24, 16, 16, 8, 8, 8, 8, 12, 12)]
         + [pltpu.VMEM((beads, 12, 128), F32)] * 2
-        + [dma(4)] * 4 + [dma(beads)] * 4 + COMPUTE_SCRATCH,
+        + [dma(6)] * 4 + [dma(beads)] * 4 + COMPUTE_SCRATCH,
         compiler_params=pltpu.CompilerParams(
             collective_id=0, has_side_effects=True, vmem_limit_bytes=60 << 20
         ),
@@ -573,7 +607,7 @@
         jnp.transpose(positions, (1, 0, 2)), jnp.transpose(momenta, (1, 0, 2)), species[None], neighbours,
         send_list[None], embedding, radial_one, radial_two, mix_one, mix_two, read_one[None], read_two[None],
     )
-    return jnp.transpose(q, (1, 0, 2)), jnp.transpose(p, (1, 0, 2))
+    return jnp.transpose(out[0] + out[1], (1, 0, 2)), jnp.transpose(out[2] - out[3], (1, 0, 2))
 
 
 def solution(mesh):

time: 50.9 us -> 50 us (0.982)
  local copies, waits for them, and re-layouts: 1.97 us -> 0 us
  other arithmetic: 0 us -> 1.35 us
    unnamed x6 -> x0, local copies, waits for them, and re-layouts: 1.97 us -> none
    sub x0 -> x1, other arithmetic: none -> 1.35 us  [shards(): out[2] - out[3]]
where the time goes in v5:
time: 50 us; the launch traced here: 49.9 us
  Pallas kernels  47.9 us (96%)
  other arithmetic  1.35 us (3%)
  between operations  0.64 us (1%)
    pallas_call x1, Pallas kernels, shards(): pl.pallas_call(lambda *refs: step_kernel(domains, beads, *refs), out_shap...  47.9 us
    sub x1, other arithmetic, shards(): out[2] - out[3]  1.35 us

profile of v5, /device:TPU:1, one launch (start us, length us, event | category | flops | bytes accessed | tf_op | source)
XLA Modules:
  0.0 49.9 jit_solution(11632079127747145485)
XLA Ops:
  0.6 47.9 %md_step.1 = f32[4,3,1,512]{3,2,1,0:T(1,128)} custom-call(f32[3,1,512]{2,1,0:T(1,128)} %bitcast.10, f32[3,1,512]{2,1,0:T(1,128)} %bitcast.11, s32[1,512]{1,0:T(1,128)} %bitcast.12, s32[8,512]{1,0:T(8,128)} %refs_3_.1, s32[1,512]{1,0:T(1,128)} %bitcast.13, f32[2,128]{1,0:T(2,128)} %refs_5_.1, f32[8,128]{1,0:T(8,128)} %refs_6_.1, f32[8,128]{1,0:T(8,128)} %refs_7_.1, ...), custom_call_target="tpu_custom_call" | custom-call | tf_op jit(solution)/shard_map/md_step/pallas_call | solution.py:594
  48.5 1.4 %subtract_bitcast_fusion = (f32[1,3,512]{2,0,1:T(1,128)}, f32[1,3,512]{2,0,1:T(1,128)}) fusion(f32[4,3,1,512]{3,2,1,0:T(1,128)} %md_step.1), kind=kLoop, calls=%fused_computation | loop fusion | flops 3072 | bytes 36864 | tf_op jit(solution)/shard_map/sub | solution.py:610

commit v6 on v5

--- a/solution.py
+++ b/solution.py
@@ -428,14 +428,17 @@
 
 def step_kernel(
     domains, beads,
-    pos, mom, spec, nbr, send_ref, emb, r1, r2, mix1, mix2, rd1, rd2,
-    packed,
-    msg_up, msg_low, in_low, in_up, in_low2, in_up2,
-    to_low, to_up, to_low2, to_up2, to_low_s, to_up_s, kept,
-    from_low, from_up, from_low2, from_up2, from_low_s, from_up_s, q_src, p_src, q_all, p_all,
-    fs_sem, fr_sem, hs_sem, hr_sem, qs_sem, qr_sem, ps_sem, pr_sem,
-    *work,
+    *refs,
 ):
+    sources, packed, held, in_sem = refs[:12], refs[12], refs[13:25], refs[25]
+    (
+        msg_up, msg_low, in_low, in_up, in_low2, in_up2,
+        to_low, to_up, to_low2, to_up2, to_low_s, to_up_s, kept,
+        from_low, from_up, from_low2, from_up2, from_low_s, from_up_s, q_src, p_src, q_all, p_all,
+        fs_sem, fr_sem, hs_sem, hr_sem, qs_sem, qr_sem, ps_sem, pr_sem,
+        *work,
+    ) = refs[26:]
+    pos, mom, spec, nbr, send_ref, emb, r1, r2, mix1, mix2, rd1, rd2 = held
     me = lax.axis_index("space")
     bead = lax.axis_index("bead")
     near = [lax.rem(me + s + domains, domains) for s in (1, -1, 2, -2)]
@@ -445,6 +448,12 @@
         pl.semaphore_signal(barrier, inc=1, device_id={"space": p}, device_id_type=MESH)
     for o in range(1, beads):
         pl.semaphore_signal(barrier, inc=1, device_id={"bead": ring[o]}, device_id_type=MESH)
+
+    loads = [pltpu.make_async_copy(a, b, in_sem.at[i]) for i, (a, b) in enumerate(zip(sources, held))]
+    for c in loads:
+        c.start()
+    for c in loads:
+        c.wait()
 
     flags = spec[...].astype(F32)
     send = send_ref[...]
@@ -591,22 +600,25 @@
     domains, beads = lax.axis_size("space"), lax.axis_size("bead")
     dma = lambda n: pltpu.SemaphoreType.DMA((n,))
     rows = lambda n: pltpu.VMEM((n, 128), F32)
+    given = (
+        jnp.transpose(positions, (1, 0, 2)), jnp.transpose(momenta, (1, 0, 2)), species[None], neighbours,
+        send_list[None], embedding, radial_one, radial_two, mix_one, mix_two, read_one[None], read_two[None],
+    )
     out = pl.pallas_call(
         lambda *refs: step_kernel(domains, beads, *refs),
         out_shape=jax.ShapeDtypeStruct((4, 3, 1, 512), F32),
-        in_specs=[VM] * 12,
+        in_specs=[pl.BlockSpec(memory_space=pl.ANY)] * 12,
         out_specs=VM,
-        scratch_shapes=[rows(n) for n in (40, 40, 40, 40, 8, 8, 16, 16, 8, 8, 8, 8, 24, 16, 16, 8, 8, 8, 8, 12, 12)]
+        scratch_shapes=[pltpu.VMEM(a.shape, a.dtype) for a in given]
+        + [dma(12)]
+        + [rows(n) for n in (40, 40, 40, 40, 8, 8, 16, 16, 8, 8, 8, 8, 24, 16, 16, 8, 8, 8, 8, 12, 12)]
         + [pltpu.VMEM((beads, 12, 128), F32)] * 2
         + [dma(6)] * 4 + [dma(beads)] * 4 + COMPUTE_SCRATCH,
         compiler_params=pltpu.CompilerParams(
             collective_id=0, has_side_effects=True, vmem_limit_bytes=60 << 20
         ),
         name="md_step",
-    )(
-        jnp.transpose(positions, (1, 0, 2)), jnp.transpose(momenta, (1, 0, 2)), species[None], neighbours,
-        send_list[None], embedding, radial_one, radial_two, mix_one, mix_two, read_one[None], read_two[None],
-    )
+    )(*given)
     return jnp.transpose(out[0] + out[1], (1, 0, 2)), jnp.transpose(out[2] - out[3], (1, 0, 2))
 
 

time: 50 us -> 48.9 us (0.978)
  Pallas kernels: 47.9 us -> 46.7 us
    pallas_call x1, Pallas kernels: 47.9 us -> 46.7 us  [shards(): pl.pallas_call(lambda *refs: step_kernel(domains, beads, *refs), out_shap...]
where the time goes in v6:
time: 48.9 us; the launch traced here: 48.7 us
  Pallas kernels  46.7 us (96%)
  other arithmetic  1.35 us (3%)
  between operations  0.64 us (1%)
    pallas_call x1, Pallas kernels, shards(): pl.pallas_call(lambda *refs: step_kernel(domains, beads, *refs), out_shap...  46.7 us
    sub x1, other arithmetic, shards(): out[2] - out[3]  1.35 us

profile of v6, /device:TPU:1, one launch (start us, length us, event | category | flops | bytes accessed | tf_op | source)
XLA Modules:
  0.0 48.7 jit_solution(8314782965563870912)
XLA Ops:
  0.6 46.7 %md_step.1 = f32[4,3,1,512]{3,2,1,0:T(1,128)} custom-call(f32[3,1,512]{2,1,0:T(1,128)} %bitcast.10, f32[3,1,512]{2,1,0:T(1,128)} %bitcast.11, s32[1,512]{1,0:T(1,128)} %bitcast.12, s32[8,512]{1,0:T(8,128)} %refs_3_.1, s32[1,512]{1,0:T(1,128)} %bitcast.13, f32[2,128]{1,0:T(2,128)} %refs_5_.1, f32[8,128]{1,0:T(8,128)} %refs_6_.1, f32[8,128]{1,0:T(8,128)} %refs_7_.1, ...), custom_call_target="tpu_custom_call" | custom-call | tf_op jit(solution)/shard_map/md_step/pallas_call | solution.py:607
  47.4 1.4 %subtract_bitcast_fusion = (f32[1,3,512]{2,0,1:T(1,128)}, f32[1,3,512]{2,0,1:T(1,128)}) fusion(f32[4,3,1,512]{3,2,1,0:T(1,128)} %md_step.1), kind=kLoop, calls=%fused_computation | loop fusion | flops 3072 | bytes 36864 | tf_op jit(solution)/shard_map/sub | solution.py:622
